TPU v7x, 256 devices: a whole 4x4x8 slice. The times are simulated.
256 devices in a mesh: sector: 8 (over x, core), op: 32 (over z, y).
Axes of the slice: x: 4, y: 4, z: 8, core: 2. Of those that a mesh axis runs over, the one named last changes fastest.
Arguments:
- wavefunction: bfloat16 [16, 512, 512], P('sector', 'op'), may hold values from -6 to 6
- sector_bases: bfloat16 [16, 512, 512], P('sector', 'op'), may hold values from -1 to 1
- left_env: bfloat16 [1536, 512, 512], P(('sector', 'op')), may hold values from -0.25 to 0.25
- right_env: bfloat16 [1536, 512, 512], P(('sector', 'op')), may hold values from -0.02734375 to 0.02734375
- pair_source: int32 [1536], P(('sector', 'op')), may hold values from 0 to 15, as said below
- pair_target: int32 [1536], P(('sector', 'op')), may hold values from 0 to 15
- sector_slot: int32 [16], replicated, may hold values from 0 to 15, as said below
- orders: int32 [16], replicated, may hold values from 256 to 512, as said below
Outputs:
- sigma_blocks: bfloat16 [16, 512, 512], P('sector', 'op')
- left_rotated: bfloat16 [1536, 512, 512], P(('sector', 'op'))
Inputs may be any that keep to these rules, and one draw needn't show every extreme that they name: A permutation: sector s's blocks stand at slot sector_slot[s]. `pair_source`: the pairs held by index i of the sector axis have sources whose slots lie in i * 2 to (i + 1) * 2 - 1. `orders`: some sector has order exactly 512.
All inputs are finite; a program needn't handle non-finite values.
Results may differ from a plain program's by a relative error of at most 0.0049.
Values may be sent and summed in bfloat16 or wider, within the bound.
No kernel may reach another device: no remote copies, remote signals or barrier semaphores. Data moves between devices by JAX's collectives and lax.ppermute only.
A program may use at most 128 MiB of HBM per device.

v0:
```python
import jax
import jax.numpy as jnp
from jax import lax
from jax.sharding import PartitionSpec as P


def joined_along(tiles, dim):
    dims = list(tiles.shape[1:])
    dims[dim] *= tiles.shape[0]
    return jnp.moveaxis(tiles, 0, dim).reshape(dims)


def from_everyone(array, axis):
    copies = jnp.broadcast_to(array, (lax.axis_size(axis), *array.shape))
    return lax.all_to_all(copies, axis, split_axis=0, concat_axis=0, tiled=True)


def gather_directly(array, axis, dim):
    return joined_along(from_everyone(array, axis), dim)


def in_blocks(array, dim, size):
    before, after = (array.shape[:dim], array.shape[dim + 1 :])
    return jnp.moveaxis(array.reshape(*before, size, -1, *after), dim, 0)


def sent_and_summed(array, axis, dim):
    size = lax.axis_size(axis)
    tiles = lax.all_to_all(in_blocks(array, dim, size), axis, 0, 0, tiled=True)
    return jnp.sum(tiles, axis=0)


def slot_of(labels, sector_slot):
    sectors = sector_slot.shape[0]
    numbers = jnp.arange(sectors, dtype=jnp.int32)
    matches = labels[:, None] == numbers[None, :]
    return jnp.sum(jnp.where(matches, sector_slot[None, :], 0), axis=1)


def fold_rows(pick_source, stacked, left_env):
    chosen = jnp.einsum(
        "pq,qnk->pnk", pick_source, stacked, preferred_element_type=jnp.float32
    ).astype(jnp.bfloat16)
    return jnp.einsum("pin,pnk->pik", left_env, chosen, preferred_element_type=jnp.float32)


def per_device(
    wavefunction, sector_bases, left_env, right_env, pair_source, pair_target, sector_slot, orders
):
    sectors = sector_slot.shape[0]
    per_owner = wavefunction.shape[0]
    slab = wavefunction.shape[1]
    width = wavefunction.shape[2]
    owner_index = lax.axis_index("sector")
    row_begin = lax.axis_index("op") * slab
    numbers = jnp.arange(sectors, dtype=jnp.int32)
    placed = sector_slot[None, :] == numbers[:, None]
    slot_order = jnp.sum(jnp.where(placed, orders[None, :], 0), axis=1)
    local_order = lax.dynamic_slice_in_dim(slot_order, owner_index * per_owner, per_owner)
    columns = jnp.arange(width, dtype=jnp.int32)
    row_ids = row_begin + jnp.arange(slab, dtype=jnp.int32)
    inside = (row_ids[None, :, None] < local_order[:, None, None]) & (
        columns[None, None, :] < local_order[:, None, None]
    )
    masked = jnp.where(inside, wavefunction, jnp.zeros((), wavefunction.dtype))
    source_slot = slot_of(pair_source, sector_slot)
    target_slot = slot_of(pair_target, sector_slot)
    owner_slots = jnp.arange(per_owner, dtype=jnp.int32)
    pick_source = (source_slot[:, None] - owner_index * per_owner == owner_slots[None, :]).astype(
        jnp.bfloat16
    )
    pick_target = (target_slot[:, None] == numbers[None, :]).astype(jnp.bfloat16)
    pick_weight = pick_target.astype(jnp.float32)
    projected = fold_rows(pick_source, gather_directly(masked, "op", 1), left_env).astype(
        jnp.bfloat16
    )
    owned_bases = gather_directly(sector_bases, "op", 1)
    chosen_source = jnp.einsum(
        "pq,qkj->pkj", pick_source, owned_bases, preferred_element_type=jnp.float32
    ).astype(jnp.bfloat16)
    half_rotated = jnp.einsum(
        "pik,pkj->pij", left_env, chosen_source, preferred_element_type=jnp.float32
    ).astype(jnp.bfloat16)
    chosen_target = jnp.einsum(
        "ps,skj->pkj",
        pick_target,
        lax.all_gather(owned_bases, "sector", axis=0, tiled=True),
        preferred_element_type=jnp.float32,
    ).astype(jnp.bfloat16)
    left_rotated = jnp.einsum(
        "pra,prc->pac", chosen_target, half_rotated, preferred_element_type=jnp.float32
    ).astype(jnp.bfloat16)
    products = jnp.einsum("pik,pjk->pij", projected, right_env, preferred_element_type=jnp.float32)
    partial_value = jnp.einsum(
        "ps,pij->sij", pick_weight, products, precision=lax.Precision.HIGHEST
    )
    owner_share = lax.psum_scatter(partial_value, "sector", scatter_dimension=0, tiled=True)
    sigma_part = sent_and_summed(owner_share, "op", 1)
    sigma_blocks = jnp.where(inside, sigma_part, jnp.zeros((), jnp.float32)).astype(jnp.bfloat16)
    return (sigma_blocks, left_rotated)


def solution(mesh):
    placed = (
        P("sector", "op", None),
        P("sector", "op", None),
        P(("sector", "op"), None, None),
        P(("sector", "op"), None, None),
        P(("sector", "op")),
        P(("sector", "op")),
        P(),
        P(),
    )
    return jax.shard_map(
        per_device,
        mesh=mesh,
        in_specs=placed,
        out_specs=(P("sector", "op", None), P(("sector", "op"), None, None)),
        check_vma=False,
    )
```

profile of v0, /device:TPU:1, one launch (start us, length us, event | category | flops | bytes accessed | tf_op | source)
XLA Modules:
  0.0 277.4 jit_solution(11869266443953004230)
XLA Ops:
  7.2 0.0 copy-start
  7.2 0.9 select_reduce_fusion
  8.1 0.1 dynamic_slice.3
  8.2 0.1 iota_compare_fusion.4
  8.3 0.1 broadcast_compare_fusion
  8.4 0.9 and_select_fusion.1
  9.3 1.1 broadcast_in_dim.64
  10.4 12.2 %all-to-all-start = ((bf16[32,2,16,512]{3,2,1,0:T(8,128)(2,1)}), bf16[32,2,16,512]{3,2,1,0:T(8,128)(2,1)}, u32[]{:S(2)}, u32[]{:S(2)}) async-start(bf16[32,2,16,512]{3,2,1,0:T(8,128)(2,1)} %broadcast_in_dim.64), calls=%async_computation | async-start | bytes 2097152 | tf_op jit(solution)/shard_map/all_to_all | solution.py:15
  22.5 0.0 reduce-scatter.2.cloned.1.call-start
  22.6 0.9 select_reduce_fusion.2
  23.5 25.2 %all-to-all-done = bf16[32,2,16,512]{3,2,1,0:T(8,128)(2,1)} async-done(((bf16[32,2,16,512]{3,2,1,0:T(8,128)(2,1)}), bf16[32,2,16,512]{3,2,1,0:T(8,128)(2,1)}, u32[]{:S(2)}, u32[]{:S(2)}) %all-to-all-start) | async-done | bytes 1048608 | tf_op jit(solution)/shard_map/all_to_all | solution.py:15
  48.7 1.3 copy.27
  50.0 4.0 %convolution_convert_fusion.1 = bf16[6,512,512]{2,0,1:T(8,128)(2,1)} fusion(bf16[2,512,512]{2,1,0:T(8,128)(2,1)S(1)} %bitcast.25, s32[6]{0:T(128)S(1)} %broadcast_subtract_fusion), kind=kOutput, calls=%fused_computation.15 | convolution fusion | flops 7864332 | bytes 4194328 | tf_op jit(solution)/shard_map/pq,qnk->pnk/dot_general | solution.py:41
  54.0 0.0 copy-done
  54.0 10.6 %fusion.11 = f32[6,512,512]{2,1,0:T(8,128)} fusion(bf16[6,512,512]{2,1,0:T(8,128)(2,1)} %param.11, bf16[6,512,512]{2,1,0:T(8,128)(2,1)S(1)} %copy-done, bf16[6,512,512]{2,0,1:T(8,128)(2,1)} %convolution_convert_fusion.1), kind=kOutput, calls=%fused_computation.11 | convolution fusion | flops 3222798336 | bytes 15728640 | tf_op jit(solution)/shard_map/pik,pjk->pij/dot_general | solution.py:93
  64.6 14.2 %fusion.2 = f32[16,512,512]{2,0,1:T(8,128)S(1)} fusion(f32[6,512,512]{2,1,0:T(8,128)} %fusion.11, s32[6]{0:T(128)S(1)} %get-tuple-element.6), kind=kOutput, calls=%fused_computation.2 | convolution fusion | flops 301989984 | bytes 23068696 | tf_op jit(solution)/shard_map/ps,pij->sij/dot_general | solution.py:94
  78.8 19.3 %copy.32 = f32[16,512,512]{2,1,0:T(8,128)} copy(f32[16,512,512]{2,0,1:T(8,128)S(1)} %fusion.2) | data formatting | bytes 33554432 | tf_op jit(solution)/shard_map/ps,pij->sij/dot_general | solution.py:94
  98.1 0.0 copy-start.1
  98.1 0.0 reduce-scatter.2.cloned.1.call-update
  98.1 0.0 all-gather.2.cloned.1.call-start
  98.1 0.7 copy-done.1
  98.8 0.1 broadcast_in_dim.66
  99.0 31.6 %all_to_all.15 = bf16[32,2,16,512]{3,2,1,0:T(8,128)(2,1)S(1)} all-to-all(bf16[32,2,16,512]{3,2,1,0:T(8,128)(2,1)S(1)} %broadcast_in_dim.66), channel_id=1, replica_groups=mesh['sector'=8,'op'=32] {'op'}, dimensions={0} | all-to-all | bytes 2097152 | tf_op jit(solution)/shard_map/all_to_all | solution.py:15
  130.5 1.1 copy.34
  131.6 0.0 all-gather.2.cloned.1.call-update
  131.6 59.6 %reduce-scatter.2.cloned.1.call-done = f32[2,512,512]{2,1,0:T(8,128)} async-done(((f32[16,512,512]{2,1,0:T(8,128)}), f32[2,512,512]{2,1,0:T(8,128)}) %reduce-scatter.2.cloned.1.call-update) | async-done | bytes 2097168 | tf_op jit(solution)/shard_map/reduce_scatter | solution.py:97
  191.2 4.7 %copy.69 = f32[2,32,16,512]{3,0,2,1:T(2,128)} copy(f32[2,32,16,512]{3,2,1,0:T(8,128)} %bitcast.26) | data formatting | bytes 4194304 | tf_op jit(solution)/shard_map/reshape | solution.py:24
  195.9 9.7 %all-to-all-start.1 = ((f32[32,2,16,512]{3,1,2,0:T(2,128)}), f32[32,2,16,512]{3,1,2,0:T(2,128)}, u32[]{:S(2)}, u32[]{:S(2)}) async-start(f32[32,2,16,512]{3,1,2,0:T(2,128)} %bitcast.24), calls=%async_computation.2 | async-start | bytes 4194304 | tf_op jit(solution)/shard_map/all_to_all | solution.py:29
  205.6 4.5 %convolution_convert_fusion = bf16[6,512,512]{2,0,1:T(8,128)(2,1)} fusion(bf16[2,512,512]{2,1,0:T(8,128)(2,1)} %bitcast.23, s32[6]{0:T(128)S(1)} %broadcast_subtract_fusion), kind=kOutput, calls=%fused_computation.14 | convolution fusion | flops 7864332 | bytes 4194328 | tf_op jit(solution)/shard_map/pq,qkj->pkj/dot_general | solution.py:78
  210.1 36.4 %all-gather.2.cloned.1.call-done = bf16[16,512,512]{2,1,0:T(8,128)(2,1)} async-done(((bf16[2,512,512]{2,1,0:T(8,128)(2,1)}), bf16[16,512,512]{2,1,0:T(8,128)(2,1)}) %all-gather.2.cloned.1.call-update) | async-done | bytes 8388624 | tf_op jit(solution)/shard_map/all_gather | solution.py:87
  246.5 10.1 %fusion.13 = bf16[6,512,512]{2,0,1:T(8,128)(2,1)} fusion(bf16[16,512,512]{2,1,0:T(8,128)(2,1)} %all-gather.2.cloned.1.call-done, s32[6]{0:T(128)S(1)} %get-tuple-element.6), kind=kOutput, calls=%fused_computation.13 | convolution fusion | flops 51904608 | bytes 11534360 | tf_op jit(solution)/shard_map/ps,skj->pkj/dot_general | solution.py:84
  256.6 11.0 %fusion.16 = bf16[6,512,512]{2,1,0:T(8,128)(2,1)} fusion(bf16[6,512,512]{2,0,1:T(8,128)(2,1)} %fusion.13, bf16[6,512,512]{2,1,0:T(8,128)(2,1)S(1)} %copy-done, bf16[6,512,512]{2,0,1:T(8,128)(2,1)} %convolution_convert_fusion), kind=kOutput, calls=%fused_computation.16 | convolution fusion | flops 3224371200 | bytes 12582912 | tf_op jit(solution)/shard_map/pra,prc->pac/dot_general | solution.py:90
  267.6 0.0 all-to-all-done.1
  267.6 2.3 reduce_sum.39
  269.8 0.1 fusion.31
  269.9 0.6 copy.39
  (3 shorter events, 0.0 us)
Async XLA Ops:
  7.2 46.8 %copy-start = (bf16[6,512,512]{2,1,0:T(8,128)(2,1)S(1)}, bf16[6,512,512]{2,1,0:T(8,128)(2,1)}, u32[]{:S(2)}) copy-start(bf16[6,512,512]{2,1,0:T(8,128)(2,1)} %param.10) | copy-start | bytes 9437188
  10.4 38.3 %all-to-all-start = ((bf16[32,2,16,512]{3,2,1,0:T(8,128)(2,1)}), bf16[32,2,16,512]{3,2,1,0:T(8,128)(2,1)}, u32[]{:S(2)}, u32[]{:S(2)}) async-start(bf16[32,2,16,512]{3,2,1,0:T(8,128)(2,1)} %broadcast_in_dim.64), calls=%async_computation | async-start | bytes 2097152 | tf_op jit(solution)/shard_map/all_to_all | solution.py:15
  22.5 168.7 %reduce-scatter.2.cloned.1.call-start = ((), (), s32[]{:S(2)}) async-start(), calls=%async_computation.4 | async-start | bytes 18874368 | tf_op jit(solution)/shard_map/reduce_scatter | solution.py:97
  98.1 0.8 copy-start.1
  98.1 148.4 %all-gather.2.cloned.1.call-start = ((), (), s32[]{:S(2)}) async-start(), calls=%async_computation.5 | async-start | bytes 9437184 | tf_op jit(solution)/shard_map/all_gather | solution.py:87
  195.9 71.7 %all-to-all-start.1 = ((f32[32,2,16,512]{3,1,2,0:T(2,128)}), f32[32,2,16,512]{3,1,2,0:T(2,128)}, u32[]{:S(2)}, u32[]{:S(2)}) async-start(f32[32,2,16,512]{3,1,2,0:T(2,128)} %bitcast.24), calls=%async_computation.2 | async-start | bytes 4194304 | tf_op jit(solution)/shard_map/all_to_all | solution.py:29
Sparse Core Ops, SparseCore 0:
  98.2 92.9 reduce-scatter.1
  193.7 52.7 all-gather.1
where the time goes:
time: 278 us; the launch traced here: 277 us
  waiting for transfers between devices  121 us (44%)
  matrix products  54.4 us (20%)
  blocking collectives  31.6 us (11%)
  local copies, waits for them, and re-layouts  28.9 us (10%)
  starting transfers between devices  21.9 us (8%)
  between operations  14.1 us (5%)
  other arithmetic  5.26 us (2%)
    reduce_scatter x1, waiting for transfers between devices, per_device(): lax.psum_scatter(partial_value, 'sector', scatter_dimension=0, tiled=True)  59.6 us
    all_gather x1, waiting for transfers between devices, per_device(): lax.all_gather(owned_bases, 'sector', axis=0, tiled=True)  36.4 us
    all_to_all x1, blocking collectives, from_everyone(): return lax.all_to_all(copies, axis, split_axis=0, concat_axis=0, tiled=True)  31.6 us
    all_to_all x1, waiting for transfers between devices, from_everyone(): return lax.all_to_all(copies, axis, split_axis=0, concat_axis=0, tiled=True)  25.2 us
    dot_general x1, local copies, waits for them, and re-layouts, per_device(): jnp.einsum('ps,pij->sij', pick_weight, products, precision=lax.Precision....  19.3 us
    dot_general x1, matrix products, per_device(): jnp.einsum('ps,pij->sij', pick_weight, products, precision=lax.Precision....  14.2 us
    all_to_all x1, starting transfers between devices, from_everyone(): return lax.all_to_all(copies, axis, split_axis=0, concat_axis=0, tiled=True)  12.2 us
    dot_general x1, matrix products, per_device(): jnp.einsum('pra,prc->pac', chosen_target, half_rotated, preferred_element...  11 us
  transfers between devices with their start and end apart: 4, of which 3 were waited for; matrix products, arithmetic and copies ran while one was open for 12% of the time, Pallas kernels for 0%

commit v1 on v0

v1 whole, which is shorter than its diff:
```python
import jax
import jax.numpy as jnp
from jax import lax
from jax.experimental import pallas as pl
from jax.experimental.pallas import tpu as pltpu
from jax.sharding import PartitionSpec as P


NX, NC, NZ, NY = 4, 2, 8, 4
SLOTS = 2
SECTORS = 16
PAIRS = 6
ROWS = 16
K = 512
BF = jnp.bfloat16
F32 = jnp.float32
DIST = (1, 3, 2)


SMEM = pl.BlockSpec(memory_space=pltpu.SMEM)
ANY = pl.BlockSpec(memory_space=pl.ANY)


def shift_y(a, d):
    perm = [(z * NY + y, z * NY + (y + d) % NY) for z in range(NZ) for y in range(NY)]
    return lax.ppermute(a, "op", perm)


def shift_x(a, d):
    perm = [(x * NC + c, (x + d) % NX * NC + c) for x in range(NX) for c in range(NC)]
    return lax.ppermute(a, "sector", perm)


def swap_core(a):
    perm = [(x * NC + c, x * NC + 1 - c) for x in range(NX) for c in range(NC)]
    return lax.ppermute(a, "sector", perm)


def exchange_z(tiles):
    groups = [[z * NY + y for z in range(NZ)] for y in range(NY)]
    return lax.all_to_all(tiles, "op", 0, 0, axis_index_groups=groups, tiled=True)


def place(dev_ref):
    dev = dev_ref[0]
    x = dev // 64
    c = dev // 32 % 2
    z = dev // 4 % 8
    y = dev % 4
    return x, c, z, y


def order_of(slot, sector_slot, orders):
    found = jnp.int32(0)
    for s in range(SECTORS):
        found = jnp.where(sector_slot[s] == slot, orders[s], found)
    return found


def source_y(y, k):
    return y if k == 0 else (y + NY - DIST[k - 1]) % NY


def products_kernel(
    dev, pair_source, sector_slot, orders, w0, w1, w2, w3, left, right, o0, o1, o2, o3, wm, pb
):
    p = pl.program_id(0)
    x, c, _, y = place(dev)
    sector = x * NC + c

    @pl.when(p == 0)
    def _():
        row_in = lax.broadcasted_iota(jnp.int32, (ROWS, K), 0)
        column = lax.broadcasted_iota(jnp.int32, (ROWS, K), 1)
        for a in range(SLOTS):
            order = order_of(sector * SLOTS + a, sector_slot, orders)
            for k, w in enumerate((w0, w1, w2, w3)):
                ys = source_y(y, k)

                def body(zz, carry, w=w, a=a, ys=ys, order=order):
                    row = row_in + (zz * NY + ys) * ROWS
                    keep = (row < order) & (column < order)
                    value = w[zz, a].astype(F32)
                    wm[a, zz, ys] = jnp.where(keep, value, 0.0).astype(BF)
                    return carry

                lax.fori_loop(0, NZ, body, 0)

    a = sector_slot[pair_source[p]] - sector * SLOTS
    w = wm[a].reshape(K, K)
    projected = jnp.dot(left[0], w, preferred_element_type=F32).astype(BF)
    product = lax.dot_general(
        projected, right[0], (((1,), (1,)), ((), ())), preferred_element_type=F32
    )
    pb[...] = product.astype(BF).reshape(NZ, NY, ROWS, K)
    o0[0] = pb[:, y]
    for d, out in zip(DIST, (o1, o2, o3)):
        out[0] = pb[:, (y + d) % NY]


def products(dev, pair_source, sector_slot, orders, ws, left, right):
    whole = pl.BlockSpec((NZ, SLOTS, ROWS, K), lambda p: (0, 0, 0, 0))
    pair = pl.BlockSpec((1, K, K), lambda p: (p, 0, 0))
    out = pl.BlockSpec((1, NZ, ROWS, K), lambda p: (p, 0, 0, 0))
    return pl.pallas_call(
        products_kernel,
        grid=(PAIRS,),
        out_shape=[jax.ShapeDtypeStruct((PAIRS, NZ, ROWS, K), BF)] * 4,
        in_specs=[SMEM] * 4 + [whole] * 4 + [pair] * 2,
        out_specs=[out] * 4,
        scratch_shapes=[
            pltpu.VMEM((SLOTS, NZ, NY, ROWS, K), BF),
            pltpu.VMEM((NZ, NY, ROWS, K), BF),
        ],
        name="products",
    )(dev, pair_source, sector_slot, orders, *ws, left, right)


def join_kernel(dev, b, out):
    _, _, _, y = place(dev)
    for k in range(NY):
        ys = source_y(y, k)
        for a in range(SLOTS):
            out[a, :, ys] = b[:, k, a]


def join(dev, b):
    vm = pl.BlockSpec(memory_space=pltpu.VMEM)
    return pl.pallas_call(
        join_kernel,
        out_shape=jax.ShapeDtypeStruct((SLOTS, NZ, NY, ROWS, K), BF),
        in_specs=[SMEM, vm],
        out_specs=vm,
        name="join",
    )(dev, b)


def half_kernel(dev, pair_source, sector_slot, bases, left, out):
    p = pl.program_id(0)
    x, c, _, _ = place(dev)
    a = sector_slot[pair_source[p]] - (x * NC + c) * SLOTS
    out[0] = jnp.dot(left[0], bases[a].reshape(K, K), preferred_element_type=F32).astype(BF)


def half(dev, pair_source, sector_slot, bases, left):
    pair = pl.BlockSpec((1, K, K), lambda p: (p, 0, 0))
    whole = pl.BlockSpec((SLOTS, NZ, NY, ROWS, K), lambda p: (0, 0, 0, 0, 0))
    return pl.pallas_call(
        half_kernel,
        grid=(PAIRS,),
        out_shape=jax.ShapeDtypeStruct((PAIRS, K, K), BF),
        in_specs=[SMEM] * 3 + [whole, pair],
        out_specs=pair,
        name="half",
    )(dev, pair_source, sector_slot, bases, left)


def rotate_kernel(dev, pair_target, sector_slot, half_ref, *rest):
    tables, out, chosen, sems = rest[:8], rest[8], rest[9], rest[10]
    p = pl.program_id(0)
    x, c, _, _ = place(dev)

    @pl.when(p == 0)
    def _():
        for q in range(PAIRS):
            slot = sector_slot[pair_target[q]]
            sector = slot // SLOTS
            a = slot % SLOTS
            behind = (x + NX - sector // NC) % NX
            same = (sector % NC) == c
            for k in range(4):
                steps = 0 if k == 0 else DIST[k - 1]
                for other in range(2):
                    hit = (behind == steps) & (same if other == 0 else jnp.logical_not(same))

                    @pl.when(hit)
                    def _(k=k, other=other):
                        pltpu.make_async_copy(
                            tables[other * 4 + k].at[a], chosen.at[q], sems.at[q]
                        ).start()

    pltpu.make_async_copy(tables[0].at[0], chosen.at[p], sems.at[p]).wait()
    basis = chosen[p].reshape(K, K)
    out[0] = lax.dot_general(
        basis, half_ref[0], (((0,), (0,)), ((), ())), preferred_element_type=F32
    ).astype(BF)


def rotate(dev, pair_target, sector_slot, halves, tables):
    pair = pl.BlockSpec((1, K, K), lambda p: (p, 0, 0))
    return pl.pallas_call(
        rotate_kernel,
        grid=(PAIRS,),
        out_shape=jax.ShapeDtypeStruct((PAIRS, K, K), BF),
        in_specs=[SMEM] * 3 + [pair] + [ANY] * 8,
        out_specs=pair,
        scratch_shapes=[
            pltpu.VMEM((PAIRS, NZ, NY, ROWS, K), BF),
            pltpu.SemaphoreType.DMA((PAIRS,)),
        ],
        name="rotate",
    )(dev, pair_target, sector_slot, halves, *tables)


ZB = 2


def by_target_kernel(dev, sector_slot, t0, t1, t2, t3, g0, g1, g2, g3, mine, other, acc):
    _, c, _, _ = place(dev)
    acc[...] = jnp.zeros_like(acc)
    for t, g in zip((t0, t1, t2, t3), (g0, g1, g2, g3)):
        for p in range(PAIRS):
            slot = sector_slot[t[p]]
            acc[slot] += g[p].astype(F32)
    for j in range(8):
        base = j // 2 * 4 + j % 2
        mine[j] = acc[base + c * 2]
        other[j] = acc[base + (1 - c) * 2].astype(BF)


def by_target(dev, sector_slot, targets, gathered):
    got = pl.BlockSpec((PAIRS, ZB, ROWS, K), lambda z: (0, z, 0, 0))
    out = pl.BlockSpec((8, ZB, ROWS, K), lambda z: (0, z, 0, 0))
    return pl.pallas_call(
        by_target_kernel,
        grid=(NZ // ZB,),
        out_shape=[
            jax.ShapeDtypeStruct((8, NZ, ROWS, K), F32),
            jax.ShapeDtypeStruct((8, NZ, ROWS, K), BF),
        ],
        in_specs=[SMEM] * 6 + [got] * 4,
        out_specs=[out] * 2,
        scratch_shapes=[pltpu.VMEM((SECTORS, ZB, ROWS, K), F32)],
        name="by_target",
    )(dev, sector_slot, *targets, *gathered)


def over_cores_kernel(dev, mine, other, e0, e1, e2, e3):
    x, _, _, _ = place(dev)
    for d, out in zip((0,) + DIST, (e0, e1, e2, e3)):
        xd = (x + d) % NX
        for a in range(SLOTS):
            j = xd * SLOTS + a
            out[a] = (mine[j] + other[j].astype(F32)).astype(out.dtype)


def over_cores(dev, mine, other):
    zb = 4
    got = pl.BlockSpec((8, zb, ROWS, K), lambda z: (0, z, 0, 0))
    out = pl.BlockSpec((SLOTS, zb, ROWS, K), lambda z: (0, z, 0, 0))
    shape = (SLOTS, NZ, ROWS, K)
    return pl.pallas_call(
        over_cores_kernel,
        grid=(NZ // zb,),
        out_shape=[jax.ShapeDtypeStruct(shape, F32)] + [jax.ShapeDtypeStruct(shape, BF)] * 3,
        in_specs=[SMEM] + [got] * 2,
        out_specs=[out] * 4,
        name="over_cores",
    )(dev, mine, other)


def over_x_kernel(e0, e1, e2, e3, out):
    for a in range(SLOTS):
        total = e0[a] + e1[a].astype(F32) + e2[a].astype(F32) + e3[a].astype(F32)
        out[:, a] = total.astype(BF)


def over_x(parts):
    vm = pl.BlockSpec(memory_space=pltpu.VMEM)
    return pl.pallas_call(
        over_x_kernel,
        out_shape=jax.ShapeDtypeStruct((NZ, SLOTS, ROWS, K), BF),
        in_specs=[vm] * 4,
        out_specs=vm,
        name="over_x",
    )(*parts)


def over_z_kernel(dev, sector_slot, orders, parts, out):
    x, c, z, y = place(dev)
    row = lax.broadcasted_iota(jnp.int32, (ROWS, K), 0) + (z * NY + y) * ROWS
    column = lax.broadcasted_iota(jnp.int32, (ROWS, K), 1)
    for a in range(SLOTS):
        order = order_of((x * NC + c) * SLOTS + a, sector_slot, orders)
        total = parts[0, a].astype(F32)
        for k in range(1, NZ):
            total = total + parts[k, a].astype(F32)
        keep = (row < order) & (column < order)
        out[a] = jnp.where(keep, total, 0.0).astype(BF)


def over_z(dev, sector_slot, orders, parts):
    vm = pl.BlockSpec(memory_space=pltpu.VMEM)
    return pl.pallas_call(
        over_z_kernel,
        out_shape=jax.ShapeDtypeStruct((SLOTS, ROWS, K), BF),
        in_specs=[SMEM] * 3 + [vm],
        out_specs=vm,
        name="over_z",
    )(dev, sector_slot, orders, parts)


def spread_z(a):
    return exchange_z(jnp.broadcast_to(a, (NZ, *a.shape)))


def per_device(
    wavefunction, sector_bases, left_env, right_env, pair_source, pair_target, sector_slot, orders
):
    dev = (lax.axis_index("sector") * (NZ * NY) + lax.axis_index("op")).astype(jnp.int32)
    dev = jnp.full((1,), dev, jnp.int32)

    b_y = [sector_bases] + [shift_y(sector_bases, d) for d in DIST]
    w_z = spread_z(wavefunction)
    b_y = jnp.stack(b_y)
    b_y, w_z = lax.optimization_barrier((b_y, w_z))
    ws = [w_z] + [shift_y(w_z, d) for d in DIST]
    b_z = spread_z(b_y)
    targets = [pair_target] + [shift_y(pair_target, d) for d in DIST]

    parts = products(dev, pair_source, sector_slot, orders, ws, left_env, right_env)
    got = [parts[0]] + [shift_y(parts[1 + k], d) for k, d in enumerate(DIST)]

    owned = join(dev, b_z)
    tables = [owned] + [shift_x(owned, d) for d in DIST]
    tables = tables + [swap_core(t) for t in tables]
    halves = half(dev, pair_source, sector_slot, owned, left_env)

    mine, other = by_target(dev, sector_slot, targets, got)
    other = swap_core(other)
    e = over_cores(dev, mine, other)
    e = [e[0]] + [shift_x(e[1 + k], d) for k, d in enumerate(DIST)]
    summed = exchange_z(over_x(e))
    sigma_blocks = over_z(dev, sector_slot, orders, summed)

    left_rotated = rotate(dev, pair_target, sector_slot, halves, tables)
    return sigma_blocks, left_rotated


def solution(mesh):
    placed = (
        P("sector", "op", None),
        P("sector", "op", None),
        P(("sector", "op"), None, None),
        P(("sector", "op"), None, None),
        P(("sector", "op")),
        P(("sector", "op")),
        P(),
        P(),
    )
    return jax.shard_map(
        per_device,
        mesh=mesh,
        in_specs=placed,
        out_specs=(P("sector", "op", None), P(("sector", "op"), None, None)),
        check_vma=False,
    )
```

time: 278 us -> 208 us (0.75)
  matrix products: 54.4 us -> 0 us
  Pallas kernels: 0 us -> 37.2 us
  blocking collectives: 31.6 us -> 0 us
  starting transfers between devices: 21.9 us -> 50.5 us
  local copies, waits for them, and re-layouts: 28.9 us -> 6.52 us
  between operations: 14.1 us -> 0.91 us
  waiting for transfers between devices: 121 us -> 109 us
  other arithmetic: 5.26 us -> 0.78 us
    ppermute x0 -> x23, waiting for transfers between devices: none -> 104 us  [the longest x6 57.5 us: shift_x(): return lax.ppermute(a, 'sector', perm)]
    reduce_scatter x1 -> x0, waiting for transfers between devices: 59.6 us -> none  [per_device(): lax.psum_scatter(partial_value, 'sector', scatter_dimension=0, tiled=True)]
    dot_general x6 -> x0, matrix products: 54.4 us -> none  [the longest x1 14.2 us: per_device(): jnp.einsum('ps,pij->sij', pick_weight, products, precision=lax.Precision....]
    pallas_call x0 -> x8, Pallas kernels: none -> 37.2 us  [the longest x1 9.01 us: products(): pl.pallas_call(products_kernel, grid=(PAIRS,), out_shape=[jax.ShapeDtypeS...]
    all_gather x1 -> x0, waiting for transfers between devices: 36.4 us -> none  [per_device(): lax.all_gather(owned_bases, 'sector', axis=0, tiled=True)]
    all_to_all x1 -> x0, blocking collectives: 31.6 us -> none  [from_everyone(): return lax.all_to_all(copies, axis, split_axis=0, concat_axis=0, tiled=True)]
    ppermute x0 -> x23, starting transfers between devices: none -> 30.7 us  [the longest x12 17.2 us: shift_y(): return lax.ppermute(a, 'op', perm)]
    all_to_all x2 -> x3, waiting for transfers between devices: 25.2 us -> 5.21 us  [exchange_z(): lax.all_to_all(tiles, 'op', 0, 0, axis_index_groups=groups, tiled=True)]
  transfers between devices with their start and end apart: 4 -> 26, of which waited for: 3 -> 13; matrix products, arithmetic and copies ran while one was open for 12% -> 0% of each run, Pallas kernels for 0% -> 14%
where the time goes in v1:
time: 208 us; the launch traced here: 205 us
  waiting for transfers between devices  109 us (52%)
  starting transfers between devices  50.5 us (24%)
  Pallas kernels  37.2 us (18%)
  local copies, waits for them, and re-layouts  6.52 us (3%)
    ppermute x6, waiting for transfers between devices, shift_x(): return lax.ppermute(a, 'sector', perm)  57.5 us
    ppermute x12, waiting for transfers between devices, shift_y(): return lax.ppermute(a, 'op', perm)  46.2 us
    all_to_all x3, starting transfers between devices, exchange_z(): lax.all_to_all(tiles, 'op', 0, 0, axis_index_groups=groups, tiled=True)  19.8 us
    ppermute x12, starting transfers between devices, shift_y(): return lax.ppermute(a, 'op', perm)  17.2 us
    pallas_call x1, Pallas kernels, products(): pl.pallas_call(products_kernel, grid=(PAIRS,), out_shape=[jax.ShapeDtypeS...  9.01 us
    pallas_call x1, Pallas kernels, rotate(): pl.pallas_call(rotate_kernel, grid=(PAIRS,), out_shape=jax.ShapeDtypeStru...  7.69 us
    ppermute x6, starting transfers between devices, shift_x(): return lax.ppermute(a, 'sector', perm)  7.27 us
    pallas_call x1, Pallas kernels, half(): pl.pallas_call(half_kernel, grid=(PAIRS,), out_shape=jax.ShapeDtypeStruct...  6.75 us
  transfers between devices with their start and end apart: 26, of which 13 were waited for; matrix products, arithmetic and copies ran while one was open for 0% of the time, Pallas kernels for 14%

profile of v1, /device:TPU:1, one launch (start us, length us, event | category | flops | bytes accessed | tf_op | source)
XLA Modules:
  0.0 204.8 jit_solution(6520704877820818494)
XLA Ops:
  0.6 1.5 broadcast_in_dim.10
  2.1 9.0 %all-to-all-start = ((bf16[8,2,16,512]{3,2,1,0:T(8,128)(2,1)}), bf16[8,2,16,512]{3,2,1,0:T(8,128)(2,1)S(1)}, u32[]{:S(2)}, u32[]{:S(2)}) async-start(bf16[8,2,16,512]{3,2,1,0:T(8,128)(2,1)} %broadcast_in_dim.10), calls=%async_computation | async-start | bytes 524288 | tf_op jit(solution)/shard_map/all_to_all | solution.py:41
  11.1 1.3 collective-permute-start.3
  12.4 2.6 %collective-permute-start.5 = (bf16[2,16,512]{2,1,0:T(8,128)(2,1)}, bf16[2,16,512]{2,1,0:T(8,128)(2,1)S(1)}, u32[]{:S(2)}, u32[]{:S(2)}) collective-permute-start(bf16[2,16,512]{2,1,0:T(8,128)(2,1)} %param.9), channel_id=1, source_target_pairs={{0,2},{1,3},{2,0},{3,1},{4,6},{5,7},{6,4},{7,5},{8,10},{9,11},{10,... | collective-permute-start | bytes 98312 | tf_op jit(solution)/shard_map/ppermute | solution.py:26
  15.0 1.1 collective-permute-start.4
  16.1 0.9 collective-permute-done.5
  17.0 1.3 collective-permute-done.4
  18.3 0.8 pad_maximum_fusion
  19.1 2.5 %all-to-all-done.w0 = bf16[8,2,16,512]{3,2,1,0:T(8,128)(2,1)S(1)} async-done(((bf16[8,2,16,512]{3,2,1,0:T(8,128)(2,1)}), bf16[8,2,16,512]{3,2,1,0:T(8,128)(2,1)S(1)}, u32[]{:S(2)}, u32[]{:S(2)}) %all-to-all-start) | async-done | bytes 262176 | tf_op jit(solution)/shard_map/all_to_all | solution.py:41
  21.6 1.1 broadcast_in_dim.11
  22.7 4.3 %all-to-all-start.2 = ((bf16[8,4,2,16,512]{4,3,2,1,0:T(8,128)(2,1)}), bf16[8,4,2,16,512]{4,3,2,1,0:T(8,128)(2,1)S(1)}, u32[]{:S(2)}, u32[]{:S(2)}) async-start(bf16[8,4,2,16,512]{4,3,2,1,0:T(8,128)(2,1)} %broadcast_in_dim.11), calls=%async_computation.2 | async-start | bytes 2097152 | tf_op jit(solution)/shard_map/all_to_all | solution.py:41
  27.1 2.2 %collective-permute-start.8 = (bf16[8,2,16,512]{3,2,1,0:T(8,128)(2,1)S(1)}, bf16[8,2,16,512]{3,2,1,0:T(8,128)(2,1)S(1)}, u32[]{:S(2)}, u32[]{:S(2)}) collective-permute-start(bf16[8,2,16,512]{3,2,1,0:T(8,128)(2,1)S(1)} %all-to-all-done.w0), channel_id=1, source_target_pairs={{0,2},{1,3},{2,0},{3,1},{4,6},{5,7},{6,4},{7,5},{8,10},{9,11},{10,... | collective-permute-start | bytes 786440 | tf_op jit(solution)/shard_map/ppermute | solution.py:26
  29.3 0.8 collective-permute-start.7
  30.1 0.7 collective-permute-start.6
  30.8 3.0 %collective-permute-done.8.w3 = bf16[8,2,16,512]{3,2,1,0:T(8,128)(2,1)S(1)} collective-permute-done((bf16[8,2,16,512]{3,2,1,0:T(8,128)(2,1)S(1)}, bf16[8,2,16,512]{3,2,1,0:T(8,128)(2,1)S(1)}, u32[]{:S(2)}, u32[]{:S(2)}) %collective-permute-start.8) | collective-permute-done | bytes 262176 | tf_op jit(solution)/shard_map/ppermute | solution.py:26
  33.8 7.3 %collective-permute-done.7.w2 = bf16[8,2,16,512]{3,2,1,0:T(8,128)(2,1)S(1)} collective-permute-done((bf16[8,2,16,512]{3,2,1,0:T(8,128)(2,1)S(1)}, bf16[8,2,16,512]{3,2,1,0:T(8,128)(2,1)S(1)}, u32[]{:S(2)}, u32[]{:S(2)}) %collective-permute-start.7) | collective-permute-done | bytes 262176 | tf_op jit(solution)/shard_map/ppermute | solution.py:26
  41.1 0.7 copy-done.10
  41.9 9.0 %products.1 = (bf16[6,8,16,512]{3,2,1,0:T(8,128)(2,1)}, bf16[6,8,16,512]{3,2,1,0:T(8,128)(2,1)}, bf16[6,8,16,512]{3,2,1,0:T(8,128)(2,1)}, bf16[6,8,16,512]{3,2,1,0:T(8,128)(2,1)}) custom-call(s32[1]{0:T(128)} %bitcast.dev, s32[6]{0:T(128)} %pair_source.3, s32[16]{0:T(128)} %sector_slot.9, s32[16]{0:T(128)} %orders.3, bf16[8,2,16,512]{3,2,1,0:T(8,128)(2,1)} %copy-done.4, ...), custom_call_target="tpu_custom_call" | custom-call | tf_op jit(solution)/shard_map/products/pallas_call | solution.py:105
  50.9 1.4 collective-permute-start.9
  52.3 2.1 %collective-permute-start.10 = (bf16[6,8,16,512]{3,2,1,0:T(8,128)(2,1)}, bf16[6,8,16,512]{3,2,1,0:T(8,128)(2,1)S(1)}, u32[]{:S(2)}, u32[]{:S(2)}) collective-permute-start(bf16[6,8,16,512]{3,2,1,0:T(8,128)(2,1)} %get-tuple-element.17), channel_id=1, source_target_pairs={{0,3},{1,0},{2,1},{3,2},{4,7},{5,4},{6,5},{7,6},{8,11},{9,8},{10,9... | collective-permute-start | bytes 2359304 | tf_op jit(solution)/shard_map/ppermute | solution.py:26
  54.5 1.1 collective-permute-start.11
  55.6 1.9 collective-permute-start.2
  57.4 1.4 collective-permute-start.1
  58.8 30.6 %collective-permute-done.2.t3 = s32[6]{0:T(128)S(1)} collective-permute-done((s32[6]{0:T(128)S(1)}, s32[6]{0:T(128)S(1)}, u32[]{:S(2)}, u32[]{:S(2)}) %collective-permute-start.2) | collective-permute-done | bytes 56 | tf_op jit(solution)/shard_map/ppermute | solution.py:26
  90.0 3.0 %collective-permute-done.t1 = s32[6]{0:T(128)S(1)} collective-permute-done((s32[6]{0:T(128)S(1)}, s32[6]{0:T(128)S(1)}, u32[]{:S(2)}, u32[]{:S(2)}) %collective-permute-start) | collective-permute-done | bytes 56 | tf_op jit(solution)/shard_map/ppermute | solution.py:26
  94.5 5.0 %by_target.1 = (f32[8,8,16,512]{3,2,1,0:T(8,128)}, bf16[8,8,16,512]{3,2,1,0:T(8,128)(2,1)}) custom-call(s32[1]{0:T(128)} %bitcast.dev, s32[16]{0:T(128)} %sector_slot.9, s32[6]{0:T(128)} %pair_target.1, s32[6]{0:T(128)} %copy-done.16, s32[6]{0:T(128)} %copy-done.15, s32[6]{0:T(128)} %copy-done.14, bf16[6,8,16,512]{3,2,1,0:T(8,128)(2,1)} %get-tuple-element.15.g0, ...), custom_call_target="tpu_custom_call" | custom-call | tf_op jit(solution)/shard_map/by_target/pallas_call | solution.py:224
  99.5 2.9 %collective-permute-start.12 = (bf16[8,8,16,512]{3,2,1,0:T(8,128)(2,1)}, bf16[8,8,16,512]{3,2,1,0:T(8,128)(2,1)}, u32[]{:S(2)}, u32[]{:S(2)}) collective-permute-start(bf16[8,8,16,512]{3,2,1,0:T(8,128)(2,1)} %get-tuple-element.20), channel_id=1, source_target_pairs={{0,32},{32,0},{64,96},{96,64},{128,160},{160,128},{192,224},{224,1... | collective-permute-start | bytes 3145736 | tf_op jit(solution)/shard_map/ppermute | solution.py:36
  102.4 1.0 copy-done.1
  103.4 2.3 %join.1.bases.rest_0_ = bf16[2,8,4,16,512]{4,3,2,1,0:T(8,128)(2,1)} custom-call(s32[1]{0:T(128)} %bitcast.dev, bf16[8,4,2,16,512]{4,3,2,1,0:T(8,128)(2,1)} %copy-done.1), custom_call_target="tpu_custom_call" | custom-call | tf_op jit(solution)/shard_map/join/pallas_call | solution.py:129
  105.7 2.7 %collective-permute-start.18 = (bf16[2,8,4,16,512]{4,3,2,1,0:T(8,128)(2,1)}, bf16[2,8,4,16,512]{4,3,2,1,0:T(8,128)(2,1)S(1)}, u32[]{:S(2)}, u32[]{:S(2)}) collective-permute-start(bf16[2,8,4,16,512]{4,3,2,1,0:T(8,128)(2,1)} %join.1.bases.rest_0_), channel_id=1, source_target_pairs={{0,128},{32,160},{64,192},{96,224},{128,0},{160,32},{192,64},{224,... | collective-permute-start | bytes 3145736 | tf_op jit(solution)/shard_map/ppermute | solution.py:31
  108.4 0.9 collective-permute-start.17
  109.9 2.8 %over_cores.1 = (f32[2,8,16,512]{3,2,1,0:T(8,128)}, bf16[2,8,16,512]{3,2,1,0:T(8,128)(2,1)}, bf16[2,8,16,512]{3,2,1,0:T(8,128)(2,1)}, bf16[2,8,16,512]{3,2,1,0:T(8,128)(2,1)}) custom-call(s32[1]{0:T(128)} %bitcast.dev, f32[8,8,16,512]{3,2,1,0:T(8,128)} %get-tuple-element.19.mine, bf16[8,8,16,512]{3,2,1,0:T(8,128)(2,1)} %collective-permute-done.12.other), custom_call_target="tpu_custom_call" | custom-call | tf_op jit(solution)/shard_map/over_cores/pallas_call | solution.py:252
  113.0 1.1 collective-permute-start.19
  114.2 18.0 %collective-permute-done.18.rest_3_ = bf16[2,8,4,16,512]{4,3,2,1,0:T(8,128)(2,1)S(1)} collective-permute-done((bf16[2,8,4,16,512]{4,3,2,1,0:T(8,128)(2,1)}, bf16[2,8,4,16,512]{4,3,2,1,0:T(8,128)(2,1)S(1)}, u32[]{:S(2)}, u32[]{:S(2)}) %collective-permute-start.18) | collective-permute-done | bytes 1048608 | tf_op jit(solution)/shard_map/ppermute | solution.py:31
  132.1 1.3 collective-permute-start.22
  133.5 21.3 %collective-permute-done.17.rest_2_ = bf16[2,8,4,16,512]{4,3,2,1,0:T(8,128)(2,1)S(1)} collective-permute-done((bf16[2,8,4,16,512]{4,3,2,1,0:T(8,128)(2,1)}, bf16[2,8,4,16,512]{4,3,2,1,0:T(8,128)(2,1)S(1)}, u32[]{:S(2)}, u32[]{:S(2)}) %collective-permute-start.17) | collective-permute-done | bytes 1048608 | tf_op jit(solution)/shard_map/ppermute | solution.py:31
  154.8 0.8 collective-permute-start.21
  155.7 4.9 %collective-permute-done.13.e1 = bf16[2,8,16,512]{3,2,1,0:T(8,128)(2,1)S(1)} collective-permute-done((bf16[2,8,16,512]{3,2,1,0:T(8,128)(2,1)}, bf16[2,8,16,512]{3,2,1,0:T(8,128)(2,1)S(1)}, u32[]{:S(2)}, u32[]{:S(2)}) %collective-permute-start.13) | collective-permute-done | bytes 262176 | tf_op jit(solution)/shard_map/ppermute | solution.py:31
  160.6 7.7 %collective-permute-done.14.e2 = bf16[2,8,16,512]{3,2,1,0:T(8,128)(2,1)} collective-permute-done((bf16[2,8,16,512]{3,2,1,0:T(8,128)(2,1)}, bf16[2,8,16,512]{3,2,1,0:T(8,128)(2,1)}, u32[]{:S(2)}, u32[]{:S(2)}) %collective-permute-start.14) | collective-permute-done | bytes 262176 | tf_op jit(solution)/shard_map/ppermute | solution.py:31
  168.3 2.7 %collective-permute-start.15 = (bf16[2,8,16,512]{3,2,1,0:T(8,128)(2,1)}, bf16[2,8,16,512]{3,2,1,0:T(8,128)(2,1)}, u32[]{:S(2)}, u32[]{:S(2)}) collective-permute-start(bf16[2,8,16,512]{3,2,1,0:T(8,128)(2,1)} %get-tuple-element.24), channel_id=1, source_target_pairs={{0,128},{32,160},{64,192},{96,224},{128,0},{160,32},{192,64},{224,... | collective-permute-start | bytes 786440 | tf_op jit(solution)/shard_map/ppermute | solution.py:31
  171.0 5.6 %collective-permute-done.15.e3 = bf16[2,8,16,512]{3,2,1,0:T(8,128)(2,1)} collective-permute-done((bf16[2,8,16,512]{3,2,1,0:T(8,128)(2,1)}, bf16[2,8,16,512]{3,2,1,0:T(8,128)(2,1)}, u32[]{:S(2)}, u32[]{:S(2)}) %collective-permute-start.15) | collective-permute-done | bytes 262176 | tf_op jit(solution)/shard_map/ppermute | solution.py:31
  176.6 2.1 %over_x.1 = bf16[8,2,16,512]{3,2,1,0:T(8,128)(2,1)} custom-call(f32[2,8,16,512]{3,2,1,0:T(8,128)} %get-tuple-element.21.e0, bf16[2,8,16,512]{3,2,1,0:T(8,128)(2,1)} %copy-done.12, bf16[2,8,16,512]{3,2,1,0:T(8,128)(2,1)} %collective-permute-done.14.e2, bf16[2,8,16,512]{3,2,1,0:T(8,128)(2,1)} %collective-permute-done.15.e3), custom_call_target="tpu_custom_call" | custom-call | tf_op jit(solution)/shard_map/over_x/pallas_call | solution.py:270
  178.7 6.5 %all-to-all-start.1 = ((bf16[8,2,16,512]{3,2,1,0:T(8,128)(2,1)}), bf16[8,2,16,512]{3,2,1,0:T(8,128)(2,1)S(1)}, u32[]{:S(2)}, u32[]{:S(2)}) async-start(bf16[8,2,16,512]{3,2,1,0:T(8,128)(2,1)} %over_x.1), calls=%async_computation.1 | async-start | bytes 524288 | tf_op jit(solution)/shard_map/all_to_all | solution.py:41
  185.1 6.7 %half.1.half_ref = bf16[6,512,512]{2,1,0:T(8,128)(2,1)} custom-call(s32[1]{0:T(128)} %bitcast.dev, s32[6]{0:T(128)} %pair_source.3, s32[16]{0:T(128)} %sector_slot.9, bf16[2,8,4,16,512]{4,3,2,1,0:T(8,128)(2,1)} %join.1.bases.rest_0_, bf16[6,512,512]{2,1,0:T(8,128)(2,1)} %left.3), custom_call_target="tpu_custom_call" | custom-call | tf_op jit(solution)/shard_map/half/pallas_call | solution.py:148
  191.9 2.7 %all-to-all-done.1.parts = bf16[8,2,16,512]{3,2,1,0:T(8,128)(2,1)S(1)} async-done(((bf16[8,2,16,512]{3,2,1,0:T(8,128)(2,1)}), bf16[8,2,16,512]{3,2,1,0:T(8,128)(2,1)S(1)}, u32[]{:S(2)}, u32[]{:S(2)}) %all-to-all-start.1) | async-done | bytes 262176 | tf_op jit(solution)/shard_map/all_to_all | solution.py:41
  194.6 0.7 copy-done.5
  195.3 1.6 over_z.1
  196.9 7.7 %rotate.1 = bf16[6,512,512]{2,1,0:T(8,128)(2,1)} custom-call(s32[1]{0:T(128)} %bitcast.dev, s32[6]{0:T(128)} %pair_target.1, s32[16]{0:T(128)} %sector_slot.9, bf16[6,512,512]{2,1,0:T(8,128)(2,1)} %half.1.half_ref, bf16[2,8,4,16,512]{4,3,2,1,0:T(8,128)(2,1)} %join.1.bases.rest_0_, bf16[2,8,4,16,512]{4,3,2,1,0:T(8,128)(2,1)} %collective-permute-done.16.rest_1_, ...), custom_call_target="tpu_custom_call" | custom-call | tf_op jit(solution)/shard_map/rotate/pallas_call | solution.py:191
  (49 shorter events, 3.1 us)
Async XLA Ops:
  2.1 19.5 %all-to-all-start = ((bf16[8,2,16,512]{3,2,1,0:T(8,128)(2,1)}), bf16[8,2,16,512]{3,2,1,0:T(8,128)(2,1)S(1)}, u32[]{:S(2)}, u32[]{:S(2)}) async-start(bf16[8,2,16,512]{3,2,1,0:T(8,128)(2,1)} %broadcast_in_dim.10), calls=%async_computation | async-start | bytes 524288 | tf_op jit(solution)/shard_map/all_to_all | solution.py:41
  11.1 5.0 %collective-permute-start.3 = (bf16[2,16,512]{2,1,0:T(8,128)(2,1)}, bf16[2,16,512]{2,1,0:T(8,128)(2,1)S(1)}, u32[]{:S(2)}, u32[]{:S(2)}) collective-permute-start(bf16[2,16,512]{2,1,0:T(8,128)(2,1)} %param.9), channel_id=1, source_target_pairs={{0,1},{1,2},{2,3},{3,0},{4,5},{5,6},{6,7},{7,4},{8,9},{9,10},{10,1... | collective-permute-start | bytes 98312 | tf_op jit(solution)/shard_map/ppermute | solution.py:26
  12.4 4.6 %collective-permute-start.5 = (bf16[2,16,512]{2,1,0:T(8,128)(2,1)}, bf16[2,16,512]{2,1,0:T(8,128)(2,1)S(1)}, u32[]{:S(2)}, u32[]{:S(2)}) collective-permute-start(bf16[2,16,512]{2,1,0:T(8,128)(2,1)} %param.9), channel_id=1, source_target_pairs={{0,2},{1,3},{2,0},{3,1},{4,6},{5,7},{6,4},{7,5},{8,10},{9,11},{10,... | collective-permute-start | bytes 98312 | tf_op jit(solution)/shard_map/ppermute | solution.py:26
  15.0 3.3 %collective-permute-start.4 = (bf16[2,16,512]{2,1,0:T(8,128)(2,1)}, bf16[2,16,512]{2,1,0:T(8,128)(2,1)S(1)}, u32[]{:S(2)}, u32[]{:S(2)}) collective-permute-start(bf16[2,16,512]{2,1,0:T(8,128)(2,1)} %param.9), channel_id=1, source_target_pairs={{0,3},{1,0},{2,1},{3,2},{4,7},{5,4},{6,5},{7,6},{8,11},{9,8},{10,9... | collective-permute-start | bytes 98312 | tf_op jit(solution)/shard_map/ppermute | solution.py:26
  21.6 19.5 %copy-start.4 = (bf16[8,2,16,512]{3,2,1,0:T(8,128)(2,1)}, bf16[8,2,16,512]{3,2,1,0:T(8,128)(2,1)S(1)}, u32[]{:S(2)}) copy-start(bf16[8,2,16,512]{3,2,1,0:T(8,128)(2,1)S(1)} %all-to-all-done.w0) | copy-start | bytes 786436
  22.7 79.7 %all-to-all-start.2 = ((bf16[8,4,2,16,512]{4,3,2,1,0:T(8,128)(2,1)}), bf16[8,4,2,16,512]{4,3,2,1,0:T(8,128)(2,1)S(1)}, u32[]{:S(2)}, u32[]{:S(2)}) async-start(bf16[8,4,2,16,512]{4,3,2,1,0:T(8,128)(2,1)} %broadcast_in_dim.11), calls=%async_computation.2 | async-start | bytes 2097152 | tf_op jit(solution)/shard_map/all_to_all | solution.py:41
  27.1 6.7 %collective-permute-start.8 = (bf16[8,2,16,512]{3,2,1,0:T(8,128)(2,1)S(1)}, bf16[8,2,16,512]{3,2,1,0:T(8,128)(2,1)S(1)}, u32[]{:S(2)}, u32[]{:S(2)}) collective-permute-start(bf16[8,2,16,512]{3,2,1,0:T(8,128)(2,1)S(1)} %all-to-all-done.w0), channel_id=1, source_target_pairs={{0,2},{1,3},{2,0},{3,1},{4,6},{5,7},{6,4},{7,5},{8,10},{9,11},{10,... | collective-permute-start | bytes 786440 | tf_op jit(solution)/shard_map/ppermute | solution.py:26
  29.3 11.8 %collective-permute-start.7 = (bf16[8,2,16,512]{3,2,1,0:T(8,128)(2,1)S(1)}, bf16[8,2,16,512]{3,2,1,0:T(8,128)(2,1)S(1)}, u32[]{:S(2)}, u32[]{:S(2)}) collective-permute-start(bf16[8,2,16,512]{3,2,1,0:T(8,128)(2,1)S(1)} %all-to-all-done.w0), channel_id=1, source_target_pairs={{0,3},{1,0},{2,1},{3,2},{4,7},{5,4},{6,5},{7,6},{8,11},{9,8},{10,9... | collective-permute-start | bytes 786440 | tf_op jit(solution)/shard_map/ppermute | solution.py:26
  30.1 11.0 %collective-permute-start.6 = (bf16[8,2,16,512]{3,2,1,0:T(8,128)(2,1)S(1)}, bf16[8,2,16,512]{3,2,1,0:T(8,128)(2,1)S(1)}, u32[]{:S(2)}, u32[]{:S(2)}) collective-permute-start(bf16[8,2,16,512]{3,2,1,0:T(8,128)(2,1)S(1)} %all-to-all-done.w0), channel_id=1, source_target_pairs={{0,1},{1,2},{2,3},{3,0},{4,5},{5,6},{6,7},{7,4},{8,9},{9,10},{10,1... | collective-permute-start | bytes 786440 | tf_op jit(solution)/shard_map/ppermute | solution.py:26
  33.8 7.3 %copy-start.9 = (bf16[8,2,16,512]{3,2,1,0:T(8,128)(2,1)}, bf16[8,2,16,512]{3,2,1,0:T(8,128)(2,1)S(1)}, u32[]{:S(2)}) copy-start(bf16[8,2,16,512]{3,2,1,0:T(8,128)(2,1)S(1)} %collective-permute-done.8.w3) | copy-start | bytes 786436
  41.1 0.7 copy-start.10
  41.1 0.8 copy-start.11
  41.9 13.7 %copy-start.13 = (s32[6]{0:T(128)S(1)}, s32[6]{0:T(128)}, u32[]{:S(2)}) copy-start(s32[6]{0:T(128)} %pair_target.1) | copy-start | bytes 76
  50.9 42.2 %collective-permute-start.9 = (bf16[6,8,16,512]{3,2,1,0:T(8,128)(2,1)}, bf16[6,8,16,512]{3,2,1,0:T(8,128)(2,1)S(1)}, u32[]{:S(2)}, u32[]{:S(2)}) collective-permute-start(bf16[6,8,16,512]{3,2,1,0:T(8,128)(2,1)} %get-tuple-element.16), channel_id=1, source_target_pairs={{0,1},{1,2},{2,3},{3,0},{4,5},{5,6},{6,7},{7,4},{8,9},{9,10},{10,1... | collective-permute-start | bytes 2359304 | tf_op jit(solution)/shard_map/ppermute | solution.py:26
  52.3 40.7 %collective-permute-start.10 = (bf16[6,8,16,512]{3,2,1,0:T(8,128)(2,1)}, bf16[6,8,16,512]{3,2,1,0:T(8,128)(2,1)S(1)}, u32[]{:S(2)}, u32[]{:S(2)}) collective-permute-start(bf16[6,8,16,512]{3,2,1,0:T(8,128)(2,1)} %get-tuple-element.17), channel_id=1, source_target_pairs={{0,3},{1,0},{2,1},{3,2},{4,7},{5,4},{6,5},{7,6},{8,11},{9,8},{10,9... | collective-permute-start | bytes 2359304 | tf_op jit(solution)/shard_map/ppermute | solution.py:26
  54.5 38.6 %collective-permute-start.11 = (bf16[6,8,16,512]{3,2,1,0:T(8,128)(2,1)}, bf16[6,8,16,512]{3,2,1,0:T(8,128)(2,1)S(1)}, u32[]{:S(2)}, u32[]{:S(2)}) collective-permute-start(bf16[6,8,16,512]{3,2,1,0:T(8,128)(2,1)} %get-tuple-element.18), channel_id=1, source_target_pairs={{0,2},{1,3},{2,0},{3,1},{4,6},{5,7},{6,4},{7,5},{8,10},{9,11},{10,... | collective-permute-start | bytes 2359304 | tf_op jit(solution)/shard_map/ppermute | solution.py:26
  55.6 33.9 %collective-permute-start.2 = (s32[6]{0:T(128)S(1)}, s32[6]{0:T(128)S(1)}, u32[]{:S(2)}, u32[]{:S(2)}) collective-permute-start(s32[6]{0:T(128)S(1)} %copy-done.13), channel_id=1, source_target_pairs={{0,2},{1,3},{2,0},{3,1},{4,6},{5,7},{6,4},{7,5},{8,10},{9,11},{10,... | collective-permute-start | bytes 80 | tf_op jit(solution)/shard_map/ppermute | solution.py:26
  57.4 32.6 %collective-permute-start.1 = (s32[6]{0:T(128)S(1)}, s32[6]{0:T(128)S(1)}, u32[]{:S(2)}, u32[]{:S(2)}) collective-permute-start(s32[6]{0:T(128)S(1)} %copy-done.13), channel_id=1, source_target_pairs={{0,3},{1,0},{2,1},{3,2},{4,7},{5,4},{6,5},{7,6},{8,11},{9,8},{10,9... | collective-permute-start | bytes 80 | tf_op jit(solution)/shard_map/ppermute | solution.py:26
  89.4 3.7 %copy-start.14 = (s32[6]{0:T(128)}, s32[6]{0:T(128)S(1)}, u32[]{:S(2)}) copy-start(s32[6]{0:T(128)S(1)} %collective-permute-done.2.t3) | copy-start | bytes 76
  89.4 3.6 %collective-permute-start = (s32[6]{0:T(128)S(1)}, s32[6]{0:T(128)S(1)}, u32[]{:S(2)}, u32[]{:S(2)}) collective-permute-start(s32[6]{0:T(128)S(1)} %copy-done.13), channel_id=1, source_target_pairs={{0,1},{1,2},{2,3},{3,0},{4,5},{5,6},{6,7},{7,4},{8,9},{9,10},{10,1... | collective-permute-start | bytes 80 | tf_op jit(solution)/shard_map/ppermute | solution.py:26
  90.0 3.1 %copy-start.15 = (s32[6]{0:T(128)}, s32[6]{0:T(128)S(1)}, u32[]{:S(2)}) copy-start(s32[6]{0:T(128)S(1)} %collective-permute-done.1.t2) | copy-start | bytes 76
  93.1 0.5 copy-start.16
  93.1 0.9 copy-start.6
  93.1 1.1 copy-start.7
  93.1 1.4 copy-start.8
  99.5 10.4 %collective-permute-start.12 = (bf16[8,8,16,512]{3,2,1,0:T(8,128)(2,1)}, bf16[8,8,16,512]{3,2,1,0:T(8,128)(2,1)}, u32[]{:S(2)}, u32[]{:S(2)}) collective-permute-start(bf16[8,8,16,512]{3,2,1,0:T(8,128)(2,1)} %get-tuple-element.20), channel_id=1, source_target_pairs={{0,32},{32,0},{64,96},{96,64},{128,160},{160,128},{192,224},{224,1... | collective-permute-start | bytes 3145736 | tf_op jit(solution)/shard_map/ppermute | solution.py:36
  102.4 1.0 copy-start.1
  105.7 7.3 %copy-start = (bf16[2,8,4,16,512]{4,3,2,1,0:T(8,128)(2,1)S(1)}, bf16[2,8,4,16,512]{4,3,2,1,0:T(8,128)(2,1)}, u32[]{:S(2)}) copy-start(bf16[2,8,4,16,512]{4,3,2,1,0:T(8,128)(2,1)} %join.1.bases.rest_0_) | copy-start | bytes 3145732
  105.7 26.5 %collective-permute-start.18 = (bf16[2,8,4,16,512]{4,3,2,1,0:T(8,128)(2,1)}, bf16[2,8,4,16,512]{4,3,2,1,0:T(8,128)(2,1)S(1)}, u32[]{:S(2)}, u32[]{:S(2)}) collective-permute-start(bf16[2,8,4,16,512]{4,3,2,1,0:T(8,128)(2,1)} %join.1.bases.rest_0_), channel_id=1, source_target_pairs={{0,128},{32,160},{64,192},{96,224},{128,0},{160,32},{192,64},{224,... | collective-permute-start | bytes 3145736 | tf_op jit(solution)/shard_map/ppermute | solution.py:31
  108.4 46.4 %collective-permute-start.17 = (bf16[2,8,4,16,512]{4,3,2,1,0:T(8,128)(2,1)}, bf16[2,8,4,16,512]{4,3,2,1,0:T(8,128)(2,1)S(1)}, u32[]{:S(2)}, u32[]{:S(2)}) collective-permute-start(bf16[2,8,4,16,512]{4,3,2,1,0:T(8,128)(2,1)} %join.1.bases.rest_0_), channel_id=1, source_target_pairs={{0,192},{32,224},{64,0},{96,32},{128,64},{160,96},{192,128},{224,1... | collective-permute-start | bytes 3145736 | tf_op jit(solution)/shard_map/ppermute | solution.py:31
  109.3 46.3 %collective-permute-start.16 = (bf16[2,8,4,16,512]{4,3,2,1,0:T(8,128)(2,1)}, bf16[2,8,4,16,512]{4,3,2,1,0:T(8,128)(2,1)}, u32[]{:S(2)}, u32[]{:S(2)}) collective-permute-start(bf16[2,8,4,16,512]{4,3,2,1,0:T(8,128)(2,1)} %join.1.bases.rest_0_), channel_id=1, source_target_pairs={{0,64},{32,96},{64,128},{96,160},{128,192},{160,224},{192,0},{224,... | collective-permute-start | bytes 3145736 | tf_op jit(solution)/shard_map/ppermute | solution.py:31
  112.7 47.9 %collective-permute-start.13 = (bf16[2,8,16,512]{3,2,1,0:T(8,128)(2,1)}, bf16[2,8,16,512]{3,2,1,0:T(8,128)(2,1)S(1)}, u32[]{:S(2)}, u32[]{:S(2)}) collective-permute-start(bf16[2,8,16,512]{3,2,1,0:T(8,128)(2,1)} %get-tuple-element.22), channel_id=1, source_target_pairs={{0,64},{32,96},{64,128},{96,160},{128,192},{160,224},{192,0},{224,... | collective-permute-start | bytes 786440 | tf_op jit(solution)/shard_map/ppermute | solution.py:31
  113.0 83.9 %collective-permute-start.19 = (bf16[2,8,4,16,512]{4,3,2,1,0:T(8,128)(2,1)S(1)}, bf16[2,8,4,16,512]{4,3,2,1,0:T(8,128)(2,1)}, u32[]{:S(2)}, u32[]{:S(2)}) collective-permute-start(bf16[2,8,4,16,512]{4,3,2,1,0:T(8,128)(2,1)S(1)} %copy-done), channel_id=1, source_target_pairs={{0,32},{32,0},{64,96},{96,64},{128,160},{160,128},{192,224},{224,1... | collective-permute-start | bytes 3145736 | tf_op jit(solution)/shard_map/ppermute | solution.py:36
  132.1 59.7 %copy-start.2 = (bf16[2,8,4,16,512]{4,3,2,1,0:T(8,128)(2,1)}, bf16[2,8,4,16,512]{4,3,2,1,0:T(8,128)(2,1)S(1)}, u32[]{:S(2)}) copy-start(bf16[2,8,4,16,512]{4,3,2,1,0:T(8,128)(2,1)S(1)} %collective-permute-done.18.rest_3_) | copy-start | bytes 3145732
  132.1 64.8 %collective-permute-start.22 = (bf16[2,8,4,16,512]{4,3,2,1,0:T(8,128)(2,1)S(1)}, bf16[2,8,4,16,512]{4,3,2,1,0:T(8,128)(2,1)}, u32[]{:S(2)}, u32[]{:S(2)}) collective-permute-start(bf16[2,8,4,16,512]{4,3,2,1,0:T(8,128)(2,1)S(1)} %collective-permute-done.18.rest_3_), channel_id=1, source_target_pairs={{0,32},{32,0},{64,96},{96,64},{128,160},{160,128},{192,224},{224,1... | collective-permute-start | bytes 3145736 | tf_op jit(solution)/shard_map/ppermute | solution.py:36
  154.8 37.1 %copy-start.3 = (bf16[2,8,4,16,512]{4,3,2,1,0:T(8,128)(2,1)}, bf16[2,8,4,16,512]{4,3,2,1,0:T(8,128)(2,1)S(1)}, u32[]{:S(2)}) copy-start(bf16[2,8,4,16,512]{4,3,2,1,0:T(8,128)(2,1)S(1)} %collective-permute-done.17.rest_2_) | copy-start | bytes 3145732
  154.8 42.1 %collective-permute-start.21 = (bf16[2,8,4,16,512]{4,3,2,1,0:T(8,128)(2,1)S(1)}, bf16[2,8,4,16,512]{4,3,2,1,0:T(8,128)(2,1)}, u32[]{:S(2)}, u32[]{:S(2)}) collective-permute-start(bf16[2,8,4,16,512]{4,3,2,1,0:T(8,128)(2,1)S(1)} %collective-permute-done.17.rest_2_), channel_id=1, source_target_pairs={{0,32},{32,0},{64,96},{96,64},{128,160},{160,128},{192,224},{224,1... | collective-permute-start | bytes 3145736 | tf_op jit(solution)/shard_map/ppermute | solution.py:36
  155.6 41.4 %collective-permute-start.20 = (bf16[2,8,4,16,512]{4,3,2,1,0:T(8,128)(2,1)}, bf16[2,8,4,16,512]{4,3,2,1,0:T(8,128)(2,1)}, u32[]{:S(2)}, u32[]{:S(2)}) collective-permute-start(bf16[2,8,4,16,512]{4,3,2,1,0:T(8,128)(2,1)} %collective-permute-done.16.rest_1_), channel_id=1, source_target_pairs={{0,32},{32,0},{64,96},{96,64},{128,160},{160,128},{192,224},{224,1... | collective-permute-start | bytes 3145736 | tf_op jit(solution)/shard_map/ppermute | solution.py:36
  160.6 16.0 %copy-start.12 = (bf16[2,8,16,512]{3,2,1,0:T(8,128)(2,1)}, bf16[2,8,16,512]{3,2,1,0:T(8,128)(2,1)S(1)}, u32[]{:S(2)}) copy-start(bf16[2,8,16,512]{3,2,1,0:T(8,128)(2,1)S(1)} %collective-permute-done.13.e1) | copy-start | bytes 786436
  160.6 7.7 %collective-permute-start.14 = (bf16[2,8,16,512]{3,2,1,0:T(8,128)(2,1)}, bf16[2,8,16,512]{3,2,1,0:T(8,128)(2,1)}, u32[]{:S(2)}, u32[]{:S(2)}) collective-permute-start(bf16[2,8,16,512]{3,2,1,0:T(8,128)(2,1)} %get-tuple-element.23), channel_id=1, source_target_pairs={{0,192},{32,224},{64,0},{96,32},{128,64},{160,96},{192,128},{224,1... | collective-permute-start | bytes 786440 | tf_op jit(solution)/shard_map/ppermute | solution.py:31
  168.3 8.3 %collective-permute-start.15 = (bf16[2,8,16,512]{3,2,1,0:T(8,128)(2,1)}, bf16[2,8,16,512]{3,2,1,0:T(8,128)(2,1)}, u32[]{:S(2)}, u32[]{:S(2)}) collective-permute-start(bf16[2,8,16,512]{3,2,1,0:T(8,128)(2,1)} %get-tuple-element.24), channel_id=1, source_target_pairs={{0,128},{32,160},{64,192},{96,224},{128,0},{160,32},{192,64},{224,... | collective-permute-start | bytes 786440 | tf_op jit(solution)/shard_map/ppermute | solution.py:31
  178.7 15.9 %all-to-all-start.1 = ((bf16[8,2,16,512]{3,2,1,0:T(8,128)(2,1)}), bf16[8,2,16,512]{3,2,1,0:T(8,128)(2,1)S(1)}, u32[]{:S(2)}, u32[]{:S(2)}) async-start(bf16[8,2,16,512]{3,2,1,0:T(8,128)(2,1)} %over_x.1), calls=%async_computation.1 | async-start | bytes 524288 | tf_op jit(solution)/shard_map/all_to_all | solution.py:41
  194.6 0.7 copy-start.5

commit v2 on v1

--- a/solution.py
+++ b/solution.py
@@ -61,8 +61,8 @@
     return y if k == 0 else (y + NY - DIST[k - 1]) % NY
 
 
-def products_kernel(
-    dev, pair_source, sector_slot, orders, w0, w1, w2, w3, left, right, o0, o1, o2, o3, wm, pb
+def far_kernel(
+    dev, pair_source, sector_slot, orders, w0, w1, w2, w3, left, right, out, wm
 ):
     p = pl.program_id(0)
     x, c, _, y = place(dev)
@@ -76,110 +76,148 @@
             order = order_of(sector * SLOTS + a, sector_slot, orders)
             for k, w in enumerate((w0, w1, w2, w3)):
                 ys = source_y(y, k)
-
-                def body(zz, carry, w=w, a=a, ys=ys, order=order):
-                    row = row_in + (zz * NY + ys) * ROWS
-                    keep = (row < order) & (column < order)
+                for zz in range(NZ):
+                    limit = order - (zz * NY + ys) * ROWS
+                    keep = (row_in < limit) & (column < order)
                     value = w[zz, a].astype(F32)
                     wm[a, zz, ys] = jnp.where(keep, value, 0.0).astype(BF)
-                    return carry
-
-                lax.fori_loop(0, NZ, body, 0)
 
     a = sector_slot[pair_source[p]] - sector * SLOTS
-    w = wm[a].reshape(K, K)
-    projected = jnp.dot(left[0], w, preferred_element_type=F32).astype(BF)
-    product = lax.dot_general(
-        projected, right[0], (((1,), (1,)), ((), ())), preferred_element_type=F32
+    out[0] = chunk_product(left[0, :, 0].reshape(-1, K), wm[a], right[0]).reshape(NZ, ROWS, K)
+
+
+def chunk_product(rows, w, right):
+    projected = jnp.dot(rows, w.reshape(K, K), preferred_element_type=F32).astype(BF)
+    return lax.dot_general(
+        projected, right, (((1,), (1,)), ((), ())), preferred_element_type=F32
+    ).astype(BF)
+
+
+def near_kernel(dev, pair_source, sector_slot, wm, left, right, o0, o1, o3):
+    p = pl.program_id(0)
+    x, c, _, y = place(dev)
+    a = sector_slot[pair_source[p]] - (x * NC + c) * SLOTS
+    steps = (0,) + DIST[:2]
+    rows = jnp.concatenate([left[0, :, (y + d) % NY].reshape(-1, K) for d in steps], axis=0)
+    product = chunk_product(rows, wm[a], right[0])
+    part = NZ * ROWS
+    for k, out in enumerate((o0, o1, o3)):
+        out[0] = product[k * part : (k + 1) * part].reshape(NZ, ROWS, K)
+
+
+PAIR = pl.BlockSpec((1, K, K), lambda p, *_: (p, 0, 0))
+PAIR_OUT = pl.BlockSpec((1, NZ, ROWS, K), lambda p, *_: (p, 0, 0, 0))
+SLOT_WHOLE = pl.BlockSpec((SLOTS, NZ, NY, ROWS, K), lambda p, *_: (0, 0, 0, 0, 0))
+CHUNK = jax.ShapeDtypeStruct((PAIRS, NZ, ROWS, K), BF)
+
+
+def far_products(dev, pair_source, sector_slot, orders, ws, left, right):
+    whole = pl.BlockSpec((NZ, SLOTS, ROWS, K), lambda p, *_: (0, 0, 0, 0))
+    rows = pl.BlockSpec(
+        (1, NZ, 1, ROWS, K), lambda p, dev, *_: (p, 0, (dev[0] % NY + DIST[2]) % NY, 0, 0)
     )
-    pb[...] = product.astype(BF).reshape(NZ, NY, ROWS, K)
-    o0[0] = pb[:, y]
-    for d, out in zip(DIST, (o1, o2, o3)):
-        out[0] = pb[:, (y + d) % NY]
-
-
-def products(dev, pair_source, sector_slot, orders, ws, left, right):
-    whole = pl.BlockSpec((NZ, SLOTS, ROWS, K), lambda p: (0, 0, 0, 0))
+    return pl.pallas_call(
+        far_kernel,
+        out_shape=[CHUNK, jax.ShapeDtypeStruct((SLOTS, NZ, NY, ROWS, K), BF)],
+        grid_spec=pltpu.PrefetchScalarGridSpec(
+            num_scalar_prefetch=4,
+            grid=(PAIRS,),
+            in_specs=[whole] * 4 + [rows, PAIR],
+            out_specs=[PAIR_OUT, SLOT_WHOLE],
+        ),
+        name="far_products",
+    )(dev, pair_source, sector_slot, orders, *ws, left, right)
+
+
+def near_products(dev, pair_source, sector_slot, wm, left, right):
+    return pl.pallas_call(
+        near_kernel,
+        out_shape=[CHUNK] * 3,
+        grid_spec=pltpu.PrefetchScalarGridSpec(
+            num_scalar_prefetch=3,
+            grid=(PAIRS,),
+            in_specs=[
+                SLOT_WHOLE,
+                pl.BlockSpec((1, NZ, NY, ROWS, K), lambda p, *_: (p, 0, 0, 0, 0)),
+                PAIR,
+            ],
+            out_specs=[PAIR_OUT] * 3,
+        ),
+        name="near_products",
+    )(dev, pair_source, sector_slot, wm, left, right)
+
+
+def half_kernel(dev, pair_source, sector_slot, basis0, basis1, left, out, ordered):
+    p = pl.program_id(0)
+    x, c, _, y = place(dev)
+
+    @pl.when(p == 0)
+    def _():
+        for k in range(NY):
+            ordered[0, :, source_y(y, k)] = basis0[:, k]
+            ordered[1, :, source_y(y, k)] = basis1[:, 0, k]
+
+    a = sector_slot[pair_source[p]] - (x * NC + c) * SLOTS
+    out[0] = jnp.dot(left[0], ordered[a].reshape(K, K), preferred_element_type=F32).astype(BF)
+
+
+def half(dev, pair_source, sector_slot, basis0, basis1, left):
     pair = pl.BlockSpec((1, K, K), lambda p: (p, 0, 0))
-    out = pl.BlockSpec((1, NZ, ROWS, K), lambda p: (p, 0, 0, 0))
-    return pl.pallas_call(
-        products_kernel,
-        grid=(PAIRS,),
-        out_shape=[jax.ShapeDtypeStruct((PAIRS, NZ, ROWS, K), BF)] * 4,
-        in_specs=[SMEM] * 4 + [whole] * 4 + [pair] * 2,
-        out_specs=[out] * 4,
-        scratch_shapes=[
-            pltpu.VMEM((SLOTS, NZ, NY, ROWS, K), BF),
-            pltpu.VMEM((NZ, NY, ROWS, K), BF),
-        ],
-        name="products",
-    )(dev, pair_source, sector_slot, orders, *ws, left, right)
-
-
-def join_kernel(dev, b, out):
-    _, _, _, y = place(dev)
-    for k in range(NY):
-        ys = source_y(y, k)
-        for a in range(SLOTS):
-            out[a, :, ys] = b[:, k, a]
-
-
-def join(dev, b):
-    vm = pl.BlockSpec(memory_space=pltpu.VMEM)
-    return pl.pallas_call(
-        join_kernel,
-        out_shape=jax.ShapeDtypeStruct((SLOTS, NZ, NY, ROWS, K), BF),
-        in_specs=[SMEM, vm],
-        out_specs=vm,
-        name="join",
-    )(dev, b)
-
-
-def half_kernel(dev, pair_source, sector_slot, bases, left, out):
-    p = pl.program_id(0)
-    x, c, _, _ = place(dev)
-    a = sector_slot[pair_source[p]] - (x * NC + c) * SLOTS
-    out[0] = jnp.dot(left[0], bases[a].reshape(K, K), preferred_element_type=F32).astype(BF)
-
-
-def half(dev, pair_source, sector_slot, bases, left):
-    pair = pl.BlockSpec((1, K, K), lambda p: (p, 0, 0))
-    whole = pl.BlockSpec((SLOTS, NZ, NY, ROWS, K), lambda p: (0, 0, 0, 0, 0))
     return pl.pallas_call(
         half_kernel,
         grid=(PAIRS,),
         out_shape=jax.ShapeDtypeStruct((PAIRS, K, K), BF),
-        in_specs=[SMEM] * 3 + [whole, pair],
+        in_specs=[SMEM] * 3
+        + [
+            pl.BlockSpec((NZ, NY, ROWS, K), lambda p: (0, 0, 0, 0)),
+            pl.BlockSpec((NZ, 1, NY, ROWS, K), lambda p: (0, 0, 0, 0, 0)),
+            pair,
+        ],
         out_specs=pair,
+        scratch_shapes=[pltpu.VMEM((SLOTS, NZ, NY, ROWS, K), BF)],
         name="half",
-    )(dev, pair_source, sector_slot, bases, left)
+    )(dev, pair_source, sector_slot, basis0, basis1, left)
 
 
 def rotate_kernel(dev, pair_target, sector_slot, half_ref, *rest):
-    tables, out, chosen, sems = rest[:8], rest[8], rest[9], rest[10]
+    tables, out, chosen, sems = rest[:10], rest[10], rest[11], rest[12]
     p = pl.program_id(0)
-    x, c, _, _ = place(dev)
+    x, c, _, y = place(dev)
 
     @pl.when(p == 0)
     def _():
-        for q in range(PAIRS):
+        def fetch(q, carry):
             slot = sector_slot[pair_target[q]]
             sector = slot // SLOTS
             a = slot % SLOTS
             behind = (x + NX - sector // NC) % NX
-            same = (sector % NC) == c
-            for k in range(4):
-                steps = 0 if k == 0 else DIST[k - 1]
-                for other in range(2):
-                    hit = (behind == steps) & (same if other == 0 else jnp.logical_not(same))
-
-                    @pl.when(hit)
-                    def _(k=k, other=other):
-                        pltpu.make_async_copy(
-                            tables[other * 4 + k].at[a], chosen.at[q], sems.at[q]
-                        ).start()
-
-    pltpu.make_async_copy(tables[0].at[0], chosen.at[p], sems.at[p]).wait()
+            at = jnp.where(behind == 3, 2, jnp.where(behind == 2, 3, behind))
+            other = (sector % NC + c) % 2
+
+            def copy(source, k):
+                pltpu.make_async_copy(
+                    source, chosen.at[q, :, source_y(y, k)], sems.at[q]
+                ).start()
+
+            for core in range(NC):
+                mine = tables[core * 5 : core * 5 + 5]
+                for n in range(NX):
+
+                    @pl.when((other == core) & (a == 0) & (at == n))
+                    def _(table=mine[n]):
+                        for k in range(NY):
+                            copy(table.at[:, k], k)
+
+                @pl.when((other == core) & (a == 1))
+                def _(table=mine[4]):
+                    for k in range(NY):
+                        copy(table.at[:, at, k], k)
+
+            return carry
+
+        lax.fori_loop(0, PAIRS, fetch, 0)
+
+    pltpu.make_async_copy(chosen.at[p], chosen.at[p], sems.at[p]).wait()
     basis = chosen[p].reshape(K, K)
     out[0] = lax.dot_general(
         basis, half_ref[0], (((0,), (0,)), ((), ())), preferred_element_type=F32
@@ -192,7 +230,7 @@
         rotate_kernel,
         grid=(PAIRS,),
         out_shape=jax.ShapeDtypeStruct((PAIRS, K, K), BF),
-        in_specs=[SMEM] * 3 + [pair] + [ANY] * 8,
+        in_specs=[SMEM] * 3 + [pair] + [ANY] * 10,
         out_specs=pair,
         scratch_shapes=[
             pltpu.VMEM((PAIRS, NZ, NY, ROWS, K), BF),
@@ -310,21 +348,26 @@
     dev = (lax.axis_index("sector") * (NZ * NY) + lax.axis_index("op")).astype(jnp.int32)
     dev = jnp.full((1,), dev, jnp.int32)
 
+    w_z = spread_z(wavefunction)
     b_y = [sector_bases] + [shift_y(sector_bases, d) for d in DIST]
-    w_z = spread_z(wavefunction)
     b_y = jnp.stack(b_y)
     b_y, w_z = lax.optimization_barrier((b_y, w_z))
     ws = [w_z] + [shift_y(w_z, d) for d in DIST]
-    b_z = spread_z(b_y)
+    b_0 = spread_z(b_y[:, 0])
+    b_1 = b_y[:, 1]
+    b_1 = jnp.stack([b_1] + [shift_x(b_1, d) for d in DIST])
+    b_1 = spread_z(b_1)
     targets = [pair_target] + [shift_y(pair_target, d) for d in DIST]
 
-    parts = products(dev, pair_source, sector_slot, orders, ws, left_env, right_env)
-    got = [parts[0]] + [shift_y(parts[1 + k], d) for k, d in enumerate(DIST)]
-
-    owned = join(dev, b_z)
-    tables = [owned] + [shift_x(owned, d) for d in DIST]
+    left = left_env.reshape(PAIRS, NZ, NY, ROWS, K)
+    far, wm = far_products(dev, pair_source, sector_slot, orders, ws, left, right_env)
+    far = shift_y(far, 2)
+    near = near_products(dev, pair_source, sector_slot, wm, left, right_env)
+    got = [near[0], shift_y(near[1], 1), shift_y(near[2], 3), far]
+
+    tables = [b_0] + [shift_x(b_0, d) for d in DIST] + [b_1]
     tables = tables + [swap_core(t) for t in tables]
-    halves = half(dev, pair_source, sector_slot, owned, left_env)
+    halves = half(dev, pair_source, sector_slot, b_0, b_1, left_env)
 
     mine, other = by_target(dev, sector_slot, targets, got)
     other = swap_core(other)

time: 208 us -> 190 us (0.913)
  waiting for transfers between devices: 109 us -> 65.9 us
  blocking collectives: 0 us -> 19.2 us
  Pallas kernels: 37.2 us -> 42.1 us
  starting transfers between devices: 50.5 us -> 54.1 us
    ppermute x12, waiting for transfers between devices: 46.2 us -> 17.5 us  [shift_y(): return lax.ppermute(a, 'op', perm)]
    ppermute x6 -> x9, waiting for transfers between devices: 57.5 us -> 31.6 us  [shift_x(): return lax.ppermute(a, 'sector', perm)]
    all_to_all x0 -> x1, blocking collectives: none -> 19.2 us  [exchange_z(): lax.all_to_all(tiles, 'op', 0, 0, axis_index_groups=groups, tiled=True)]
    all_to_all x3, waiting for transfers between devices: 5.21 us -> 15.7 us  [exchange_z(): lax.all_to_all(tiles, 'op', 0, 0, axis_index_groups=groups, tiled=True)]
    pallas_call x2, Pallas kernels: 11.3 us -> 16.1 us  [the longest x1 8.46 us: near_products(): pl.pallas_call(near_kernel, out_shape=[CHUNK] * 3, grid_spec=pltpu.Prefet...]
    ppermute x5 -> x6, starting transfers between devices: 6.26 us -> 9.63 us  [swap_core(): return lax.ppermute(a, 'sector', perm)]
    all_to_all x3, starting transfers between devices: 19.8 us -> 17.5 us  [exchange_z(): lax.all_to_all(tiles, 'op', 0, 0, axis_index_groups=groups, tiled=True)]
    unnamed x34 -> x26, local copies, waits for them, and re-layouts: 3.9 us -> 1.7 us
  transfers between devices with their start and end apart: 26 -> 30, of which waited for: 13 -> 18; matrix products, arithmetic and copies ran while one was open for 0% -> 1% of each run, Pallas kernels for 14% -> 18%
where the time goes in v2:
time: 190 us; the launch traced here: 189 us
  waiting for transfers between devices  65.9 us (35%)
  starting transfers between devices  54.1 us (28%)
  Pallas kernels  42.1 us (22%)
  blocking collectives  19.2 us (10%)
  local copies, waits for them, and re-layouts  5.72 us (3%)
    ppermute x9, waiting for transfers between devices, shift_x(): return lax.ppermute(a, 'sector', perm)  31.6 us
    all_to_all x1, blocking collectives, exchange_z(): lax.all_to_all(tiles, 'op', 0, 0, axis_index_groups=groups, tiled=True)  19.2 us
    ppermute x12, starting transfers between devices, shift_y(): return lax.ppermute(a, 'op', perm)  18.5 us
    all_to_all x3, starting transfers between devices, exchange_z(): lax.all_to_all(tiles, 'op', 0, 0, axis_index_groups=groups, tiled=True)  17.5 us
    ppermute x12, waiting for transfers between devices, shift_y(): return lax.ppermute(a, 'op', perm)  17.5 us
    all_to_all x3, waiting for transfers between devices, exchange_z(): lax.all_to_all(tiles, 'op', 0, 0, axis_index_groups=groups, tiled=True)  15.7 us
    ppermute x6, starting transfers between devices, swap_core(): return lax.ppermute(a, 'sector', perm)  9.63 us
    pallas_call x1, Pallas kernels, near_products(): pl.pallas_call(near_kernel, out_shape=[CHUNK] * 3, grid_spec=pltpu.Prefet...  8.46 us
  transfers between devices with their start and end apart: 30, of which 18 were waited for; matrix products, arithmetic and copies ran while one was open for 1% of the time, Pallas kernels for 18%

profile of v2, /device:TPU:1, one launch (start us, length us, event | category | flops | bytes accessed | tf_op | source)
XLA Modules:
  0.0 188.7 jit_solution(10752365476767818726)
XLA Ops:
  0.6 1.5 broadcast_in_dim.13
  2.1 9.0 %all-to-all-start = ((bf16[8,2,16,512]{3,2,1,0:T(8,128)(2,1)}), bf16[8,2,16,512]{3,2,1,0:T(8,128)(2,1)S(1)}, u32[]{:S(2)}, u32[]{:S(2)}) async-start(bf16[8,2,16,512]{3,2,1,0:T(8,128)(2,1)} %broadcast_in_dim.13), calls=%async_computation | async-start | bytes 524288 | tf_op jit(solution)/shard_map/all_to_all | solution.py:41
  11.1 1.3 collective-permute-start.3
  12.4 2.6 %collective-permute-start.5 = (bf16[2,16,512]{2,1,0:T(8,128)(2,1)}, bf16[2,16,512]{2,1,0:T(8,128)(2,1)S(1)}, u32[]{:S(2)}, u32[]{:S(2)}) collective-permute-start(bf16[2,16,512]{2,1,0:T(8,128)(2,1)} %param.9), channel_id=1, source_target_pairs={{0,2},{1,3},{2,0},{3,1},{4,6},{5,7},{6,4},{7,5},{8,10},{9,11},{10,... | collective-permute-start | bytes 98312 | tf_op jit(solution)/shard_map/ppermute | solution.py:26
  15.0 1.1 collective-permute-start.4
  16.1 0.9 collective-permute-done.5
  17.0 1.3 collective-permute-done.4
  18.3 0.8 pad_maximum_fusion.1
  19.1 2.5 %all-to-all-done.w0 = bf16[8,2,16,512]{3,2,1,0:T(8,128)(2,1)S(1)} async-done(((bf16[8,2,16,512]{3,2,1,0:T(8,128)(2,1)}), bf16[8,2,16,512]{3,2,1,0:T(8,128)(2,1)S(1)}, u32[]{:S(2)}, u32[]{:S(2)}) %all-to-all-start) | async-done | bytes 262176 | tf_op jit(solution)/shard_map/all_to_all | solution.py:41
  21.6 2.8 %collective-permute-start.18 = (bf16[4,16,512]{2,1,0:T(8,128)(2,1)S(1)}, bf16[4,16,512]{2,1,0:T(8,128)(2,1)S(1)}, u32[]{:S(2)}, u32[]{:S(2)}) collective-permute-start(bf16[4,16,512]{2,1,0:T(8,128)(2,1)S(1)} %get-tuple-element.29), channel_id=1, source_target_pairs={{0,128},{32,160},{64,192},{96,224},{128,0},{160,32},{192,64},{224,... | collective-permute-start | bytes 196616 | tf_op jit(solution)/shard_map/ppermute | solution.py:31
  24.5 0.9 collective-permute-start.17
  26.3 1.2 collective-permute-done.17
  27.6 2.3 %collective-permute-done.16 = bf16[4,16,512]{2,1,0:T(8,128)(2,1)S(1)} collective-permute-done((bf16[4,16,512]{2,1,0:T(8,128)(2,1)S(1)}, bf16[4,16,512]{2,1,0:T(8,128)(2,1)S(1)}, u32[]{:S(2)}, u32[]{:S(2)}) %collective-permute-start.16) | collective-permute-done | bytes 65568 | tf_op jit(solution)/shard_map/ppermute | solution.py:31
  29.9 1.6 broadcast_in_dim.15
  31.5 4.5 %all-to-all-start.3 = ((bf16[8,4,4,16,512]{4,3,2,1,0:T(8,128)(2,1)}), bf16[8,4,4,16,512]{4,3,2,1,0:T(8,128)(2,1)S(1)}, u32[]{:S(2)}, u32[]{:S(2)}) async-start(bf16[8,4,4,16,512]{4,3,2,1,0:T(8,128)(2,1)} %broadcast_in_dim.15), calls=%async_computation.3 | async-start | bytes 4194304 | tf_op jit(solution)/shard_map/all_to_all | solution.py:41
  35.9 2.2 %collective-permute-start.8 = (bf16[8,2,16,512]{3,2,1,0:T(8,128)(2,1)S(1)}, bf16[8,2,16,512]{3,2,1,0:T(8,128)(2,1)S(1)}, u32[]{:S(2)}, u32[]{:S(2)}) collective-permute-start(bf16[8,2,16,512]{3,2,1,0:T(8,128)(2,1)S(1)} %all-to-all-done.w0), channel_id=1, source_target_pairs={{0,2},{1,3},{2,0},{3,1},{4,6},{5,7},{6,4},{7,5},{8,10},{9,11},{10,... | collective-permute-start | bytes 786440 | tf_op jit(solution)/shard_map/ppermute | solution.py:26
  39.5 3.1 %collective-permute-done.8.w3 = bf16[8,2,16,512]{3,2,1,0:T(8,128)(2,1)S(1)} collective-permute-done((bf16[8,2,16,512]{3,2,1,0:T(8,128)(2,1)S(1)}, bf16[8,2,16,512]{3,2,1,0:T(8,128)(2,1)S(1)}, u32[]{:S(2)}, u32[]{:S(2)}) %collective-permute-start.8) | collective-permute-done | bytes 262176 | tf_op jit(solution)/shard_map/ppermute | solution.py:26
  42.7 5.5 %collective-permute-done.7.w2 = bf16[8,2,16,512]{3,2,1,0:T(8,128)(2,1)S(1)} collective-permute-done((bf16[8,2,16,512]{3,2,1,0:T(8,128)(2,1)S(1)}, bf16[8,2,16,512]{3,2,1,0:T(8,128)(2,1)S(1)}, u32[]{:S(2)}, u32[]{:S(2)}) %collective-permute-start.7) | collective-permute-done | bytes 262176 | tf_op jit(solution)/shard_map/ppermute | solution.py:26
  49.0 7.6 %far_products.1 = (bf16[6,8,16,512]{3,2,1,0:T(8,128)(2,1)}, bf16[2,8,4,16,512]{4,3,2,1,0:T(8,128)(2,1)}) custom-call(s32[1]{0:T(128)} %bitcast.dev, s32[6]{0:T(128)} %pair_source.5, s32[16]{0:T(128)} %sector_slot.11, s32[16]{0:T(128)} %orders.3, bf16[8,2,16,512]{3,2,1,0:T(8,128)(2,1)} %copy-done.2, bf16[8,2,16,512]{3,2,1,0:T(8,128)(2,1)} %copy-done.7, ...), custom_call_target="tpu_custom_call" | custom-call | tf_op jit(solution)/shard_map/far_products/pallas_call | solution.py:119
  56.6 2.9 %collective-permute-start.11 = (bf16[6,8,16,512]{3,2,1,0:T(8,128)(2,1)}, bf16[6,8,16,512]{3,2,1,0:T(8,128)(2,1)S(1)}, u32[]{:S(2)}, u32[]{:S(2)}) collective-permute-start(bf16[6,8,16,512]{3,2,1,0:T(8,128)(2,1)} %get-tuple-element.20), channel_id=1, source_target_pairs={{0,2},{1,3},{2,0},{3,1},{4,6},{5,7},{6,4},{7,5},{8,10},{9,11},{10,... | collective-permute-start | bytes 2359304 | tf_op jit(solution)/shard_map/ppermute | solution.py:26
  59.5 8.5 %near_products.1 = (bf16[6,8,16,512]{3,2,1,0:T(8,128)(2,1)}, bf16[6,8,16,512]{3,2,1,0:T(8,128)(2,1)}, bf16[6,8,16,512]{3,2,1,0:T(8,128)(2,1)}) custom-call(s32[1]{0:T(128)} %bitcast.dev, s32[6]{0:T(128)} %pair_source.5, s32[16]{0:T(128)} %sector_slot.11, bf16[2,8,4,16,512]{4,3,2,1,0:T(8,128)(2,1)} %get-tuple-element.16.wm, ...), custom_call_target="tpu_custom_call" | custom-call | tf_op jit(solution)/shard_map/near_products/pallas_call | solution.py:133
  67.9 1.3 collective-permute-start.9
  69.2 1.4 collective-permute-start.10
  70.6 13.2 %all-to-all-done.3.basis1.rest_4_ = bf16[8,4,4,16,512]{4,3,2,1,0:T(8,128)(2,1)S(1)} async-done(((bf16[8,4,4,16,512]{4,3,2,1,0:T(8,128)(2,1)}), bf16[8,4,4,16,512]{4,3,2,1,0:T(8,128)(2,1)S(1)}, u32[]{:S(2)}, u32[]{:S(2)}) %all-to-all-start.3) | async-done | bytes 2097184 | tf_op jit(solution)/shard_map/all_to_all | solution.py:41
  83.8 0.9 broadcast_in_dim.14
  84.7 4.1 %all-to-all-start.2 = ((bf16[8,4,16,512]{3,2,1,0:T(8,128)(2,1)}), bf16[8,4,16,512]{3,2,1,0:T(8,128)(2,1)S(1)}, u32[]{:S(2)}, u32[]{:S(2)}) async-start(bf16[8,4,16,512]{3,2,1,0:T(8,128)(2,1)} %broadcast_in_dim.14), calls=%async_computation.2 | async-start | bytes 1048576 | tf_op jit(solution)/shard_map/all_to_all | solution.py:41
  88.8 3.8 %collective-permute-start.26 = (bf16[8,4,4,16,512]{4,3,2,1,0:T(8,128)(2,1)S(1)}, bf16[8,4,4,16,512]{4,3,2,1,0:T(8,128)(2,1)}, u32[]{:S(2)}, u32[]{:S(2)}) collective-permute-start(bf16[8,4,4,16,512]{4,3,2,1,0:T(8,128)(2,1)S(1)} %all-to-all-done.3.basis1.rest_4_), channel_id=1, source_target_pairs={{0,32},{32,0},{64,96},{96,64},{128,160},{160,128},{192,224},{224,1... | collective-permute-start | bytes 6291464 | tf_op jit(solution)/shard_map/ppermute | solution.py:36
  92.6 2.0 %collective-permute-start.2 = (s32[6]{0:T(128)S(1)}, s32[6]{0:T(128)S(1)}, u32[]{:S(2)}, u32[]{:S(2)}) collective-permute-start(s32[6]{0:T(128)S(1)} %copy-done.9), channel_id=1, source_target_pairs={{0,2},{1,3},{2,0},{3,1},{4,6},{5,7},{6,4},{7,5},{8,10},{9,11},{10,... | collective-permute-start | bytes 80 | tf_op jit(solution)/shard_map/ppermute | solution.py:26
  94.6 1.9 %collective-permute-done.2.t3 = s32[6]{0:T(128)S(1)} collective-permute-done((s32[6]{0:T(128)S(1)}, s32[6]{0:T(128)S(1)}, u32[]{:S(2)}, u32[]{:S(2)}) %collective-permute-start.2) | collective-permute-done | bytes 56 | tf_op jit(solution)/shard_map/ppermute | solution.py:26
  96.5 2.3 %collective-permute-start.1 = (s32[6]{0:T(128)S(1)}, s32[6]{0:T(128)S(1)}, u32[]{:S(2)}, u32[]{:S(2)}) collective-permute-start(s32[6]{0:T(128)S(1)} %copy-done.9), channel_id=1, source_target_pairs={{0,3},{1,0},{2,1},{3,2},{4,7},{5,4},{6,5},{7,6},{8,11},{9,8},{10,9... | collective-permute-start | bytes 80 | tf_op jit(solution)/shard_map/ppermute | solution.py:26
  99.6 4.1 %collective-permute-done.t1 = s32[6]{0:T(128)S(1)} collective-permute-done((s32[6]{0:T(128)S(1)}, s32[6]{0:T(128)S(1)}, u32[]{:S(2)}, u32[]{:S(2)}) %collective-permute-start) | collective-permute-done | bytes 56 | tf_op jit(solution)/shard_map/ppermute | solution.py:26
  104.6 5.0 %by_target.1 = (f32[8,8,16,512]{3,2,1,0:T(8,128)}, bf16[8,8,16,512]{3,2,1,0:T(8,128)(2,1)}) custom-call(s32[1]{0:T(128)} %bitcast.dev, s32[16]{0:T(128)} %sector_slot.11, s32[6]{0:T(128)} %pair_target.1, s32[6]{0:T(128)} %copy-done.12, s32[6]{0:T(128)} %copy-done.11, s32[6]{0:T(128)} %copy-done.10, bf16[6,8,16,512]{3,2,1,0:T(8,128)(2,1)} %get-tuple-element.17.g0, ...), custom_call_target="tpu_custom_call" | custom-call | tf_op jit(solution)/shard_map/by_target/pallas_call | solution.py:262
  109.6 3.0 %collective-permute-start.12 = (bf16[8,8,16,512]{3,2,1,0:T(8,128)(2,1)}, bf16[8,8,16,512]{3,2,1,0:T(8,128)(2,1)}, u32[]{:S(2)}, u32[]{:S(2)}) collective-permute-start(bf16[8,8,16,512]{3,2,1,0:T(8,128)(2,1)} %get-tuple-element.22), channel_id=1, source_target_pairs={{0,32},{32,0},{64,96},{96,64},{128,160},{160,128},{192,224},{224,1... | collective-permute-start | bytes 3145736 | tf_op jit(solution)/shard_map/ppermute | solution.py:36
  112.6 1.6 collective-permute-start.20
  114.2 1.0 collective-permute-done.12.other
  115.2 2.8 %over_cores.1 = (f32[2,8,16,512]{3,2,1,0:T(8,128)}, bf16[2,8,16,512]{3,2,1,0:T(8,128)(2,1)}, bf16[2,8,16,512]{3,2,1,0:T(8,128)(2,1)}, bf16[2,8,16,512]{3,2,1,0:T(8,128)(2,1)}) custom-call(s32[1]{0:T(128)} %bitcast.dev, f32[8,8,16,512]{3,2,1,0:T(8,128)} %get-tuple-element.21.mine, bf16[8,8,16,512]{3,2,1,0:T(8,128)(2,1)} %collective-permute-done.12.other), custom_call_target="tpu_custom_call" | custom-call | tf_op jit(solution)/shard_map/over_cores/pallas_call | solution.py:290
  118.1 9.4 %collective-permute-done.21.rest_3_ = bf16[8,4,16,512]{3,2,1,0:T(8,128)(2,1)S(1)} collective-permute-done((bf16[8,4,16,512]{3,2,1,0:T(8,128)(2,1)S(1)}, bf16[8,4,16,512]{3,2,1,0:T(8,128)(2,1)S(1)}, u32[]{:S(2)}, u32[]{:S(2)}) %collective-permute-start.21) | collective-permute-done | bytes 524320 | tf_op jit(solution)/shard_map/ppermute | solution.py:31
  127.5 8.8 %collective-permute-done.20.rest_2_ = bf16[8,4,16,512]{3,2,1,0:T(8,128)(2,1)} collective-permute-done((bf16[8,4,16,512]{3,2,1,0:T(8,128)(2,1)S(1)}, bf16[8,4,16,512]{3,2,1,0:T(8,128)(2,1)}, u32[]{:S(2)}, u32[]{:S(2)}) %collective-permute-start.20) | collective-permute-done | bytes 524320 | tf_op jit(solution)/shard_map/ppermute | solution.py:31
  136.2 2.4 %collective-permute-start.15 = (bf16[2,8,16,512]{3,2,1,0:T(8,128)(2,1)}, bf16[2,8,16,512]{3,2,1,0:T(8,128)(2,1)}, u32[]{:S(2)}, u32[]{:S(2)}) collective-permute-start(bf16[2,8,16,512]{3,2,1,0:T(8,128)(2,1)} %get-tuple-element.26), channel_id=1, source_target_pairs={{0,128},{32,160},{64,192},{96,224},{128,0},{160,32},{192,64},{224,... | collective-permute-start | bytes 786440 | tf_op jit(solution)/shard_map/ppermute | solution.py:31
  139.3 1.2 collective-permute-start.22
  140.5 4.7 %collective-permute-done.13.e1 = bf16[2,8,16,512]{3,2,1,0:T(8,128)(2,1)S(1)} collective-permute-done((bf16[2,8,16,512]{3,2,1,0:T(8,128)(2,1)}, bf16[2,8,16,512]{3,2,1,0:T(8,128)(2,1)S(1)}, u32[]{:S(2)}, u32[]{:S(2)}) %collective-permute-start.13) | collective-permute-done | bytes 262176 | tf_op jit(solution)/shard_map/ppermute | solution.py:31
  145.9 4.2 %collective-permute-done.15.e3 = bf16[2,8,16,512]{3,2,1,0:T(8,128)(2,1)} collective-permute-done((bf16[2,8,16,512]{3,2,1,0:T(8,128)(2,1)}, bf16[2,8,16,512]{3,2,1,0:T(8,128)(2,1)}, u32[]{:S(2)}, u32[]{:S(2)}) %collective-permute-start.15) | collective-permute-done | bytes 262176 | tf_op jit(solution)/shard_map/ppermute | solution.py:31
  150.1 1.0 collective-permute-start.23
  151.0 2.1 %over_x.1 = bf16[8,2,16,512]{3,2,1,0:T(8,128)(2,1)} custom-call(f32[2,8,16,512]{3,2,1,0:T(8,128)} %get-tuple-element.23.e0, bf16[2,8,16,512]{3,2,1,0:T(8,128)(2,1)} %copy-done.8, bf16[2,8,16,512]{3,2,1,0:T(8,128)(2,1)} %collective-permute-done.14.e2, bf16[2,8,16,512]{3,2,1,0:T(8,128)(2,1)} %collective-permute-done.15.e3), custom_call_target="tpu_custom_call" | custom-call | tf_op jit(solution)/shard_map/over_x/pallas_call | solution.py:308
  153.1 19.2 %all_to_all.20.parts = bf16[8,2,16,512]{3,2,1,0:T(8,128)(2,1)} all-to-all(bf16[8,2,16,512]{3,2,1,0:T(8,128)(2,1)} %over_x.1), channel_id=1, replica_groups={{0,4,8,12,16,20,24,28},{1,5,9,13,17,21,25,29},{2,6,10,14,18,22,26,30},{..., dimensions={0} | all-to-all | bytes 524288 | tf_op jit(solution)/shard_map/all_to_all | solution.py:41
  172.3 1.6 over_z.1
  174.0 6.8 %half.1.half_ref = bf16[6,512,512]{2,1,0:T(8,128)(2,1)} custom-call(s32[1]{0:T(128)} %bitcast.dev, s32[6]{0:T(128)} %pair_source.5, s32[16]{0:T(128)} %sector_slot.11, bf16[8,4,16,512]{3,2,1,0:T(8,128)(2,1)} %copy-done.1, bf16[8,4,4,16,512]{4,3,2,1,0:T(8,128)(2,1)} %copy-done, bf16[6,512,512]{2,1,0:T(8,128)(2,1)} %left.1), custom_call_target="tpu_custom_call" | custom-call | tf_op jit(solution)/shard_map/half/pallas_call | solution.py:166
  180.8 7.7 %rotate.1 = bf16[6,512,512]{2,1,0:T(8,128)(2,1)} custom-call(s32[1]{0:T(128)} %bitcast.dev, s32[6]{0:T(128)} %pair_target.1, s32[16]{0:T(128)} %sector_slot.11, bf16[6,512,512]{2,1,0:T(8,128)(2,1)} %half.1.half_ref, bf16[8,4,16,512]{3,2,1,0:T(8,128)(2,1)} %copy-done.1, bf16[8,4,16,512]{3,2,1,0:T(8,128)(2,1)} %collective-permute-done.19.rest_1_, ...), custom_call_target="tpu_custom_call" | custom-call | tf_op jit(solution)/shard_map/rotate/pallas_call | solution.py:229
  (53 shorter events, 6.5 us)
Async XLA Ops:
  2.1 19.5 %all-to-all-start = ((bf16[8,2,16,512]{3,2,1,0:T(8,128)(2,1)}), bf16[8,2,16,512]{3,2,1,0:T(8,128)(2,1)S(1)}, u32[]{:S(2)}, u32[]{:S(2)}) async-start(bf16[8,2,16,512]{3,2,1,0:T(8,128)(2,1)} %broadcast_in_dim.13), calls=%async_computation | async-start | bytes 524288 | tf_op jit(solution)/shard_map/all_to_all | solution.py:41
  11.1 5.0 %collective-permute-start.3 = (bf16[2,16,512]{2,1,0:T(8,128)(2,1)}, bf16[2,16,512]{2,1,0:T(8,128)(2,1)S(1)}, u32[]{:S(2)}, u32[]{:S(2)}) collective-permute-start(bf16[2,16,512]{2,1,0:T(8,128)(2,1)} %param.9), channel_id=1, source_target_pairs={{0,1},{1,2},{2,3},{3,0},{4,5},{5,6},{6,7},{7,4},{8,9},{9,10},{10,1... | collective-permute-start | bytes 98312 | tf_op jit(solution)/shard_map/ppermute | solution.py:26
  12.4 4.6 %collective-permute-start.5 = (bf16[2,16,512]{2,1,0:T(8,128)(2,1)}, bf16[2,16,512]{2,1,0:T(8,128)(2,1)S(1)}, u32[]{:S(2)}, u32[]{:S(2)}) collective-permute-start(bf16[2,16,512]{2,1,0:T(8,128)(2,1)} %param.9), channel_id=1, source_target_pairs={{0,2},{1,3},{2,0},{3,1},{4,6},{5,7},{6,4},{7,5},{8,10},{9,11},{10,... | collective-permute-start | bytes 98312 | tf_op jit(solution)/shard_map/ppermute | solution.py:26
  15.0 3.3 %collective-permute-start.4 = (bf16[2,16,512]{2,1,0:T(8,128)(2,1)}, bf16[2,16,512]{2,1,0:T(8,128)(2,1)S(1)}, u32[]{:S(2)}, u32[]{:S(2)}) collective-permute-start(bf16[2,16,512]{2,1,0:T(8,128)(2,1)} %param.9), channel_id=1, source_target_pairs={{0,3},{1,0},{2,1},{3,2},{4,7},{5,4},{6,5},{7,6},{8,11},{9,8},{10,9... | collective-permute-start | bytes 98312 | tf_op jit(solution)/shard_map/ppermute | solution.py:26
  21.6 17.2 %copy-start.2 = (bf16[8,2,16,512]{3,2,1,0:T(8,128)(2,1)}, bf16[8,2,16,512]{3,2,1,0:T(8,128)(2,1)S(1)}, u32[]{:S(2)}) copy-start(bf16[8,2,16,512]{3,2,1,0:T(8,128)(2,1)S(1)} %all-to-all-done.w0) | copy-start | bytes 786436
  21.6 4.7 %collective-permute-start.18 = (bf16[4,16,512]{2,1,0:T(8,128)(2,1)S(1)}, bf16[4,16,512]{2,1,0:T(8,128)(2,1)S(1)}, u32[]{:S(2)}, u32[]{:S(2)}) collective-permute-start(bf16[4,16,512]{2,1,0:T(8,128)(2,1)S(1)} %get-tuple-element.29), channel_id=1, source_target_pairs={{0,128},{32,160},{64,192},{96,224},{128,0},{160,32},{192,64},{224,... | collective-permute-start | bytes 196616 | tf_op jit(solution)/shard_map/ppermute | solution.py:31
  24.5 3.1 %collective-permute-start.17 = (bf16[4,16,512]{2,1,0:T(8,128)(2,1)S(1)}, bf16[4,16,512]{2,1,0:T(8,128)(2,1)S(1)}, u32[]{:S(2)}, u32[]{:S(2)}) collective-permute-start(bf16[4,16,512]{2,1,0:T(8,128)(2,1)S(1)} %get-tuple-element.29), channel_id=1, source_target_pairs={{0,192},{32,224},{64,0},{96,32},{128,64},{160,96},{192,128},{224,1... | collective-permute-start | bytes 196616 | tf_op jit(solution)/shard_map/ppermute | solution.py:31
  25.3 4.5 %collective-permute-start.16 = (bf16[4,16,512]{2,1,0:T(8,128)(2,1)S(1)}, bf16[4,16,512]{2,1,0:T(8,128)(2,1)S(1)}, u32[]{:S(2)}, u32[]{:S(2)}) collective-permute-start(bf16[4,16,512]{2,1,0:T(8,128)(2,1)S(1)} %get-tuple-element.29), channel_id=1, source_target_pairs={{0,64},{32,96},{64,128},{96,160},{128,192},{160,224},{192,0},{224,... | collective-permute-start | bytes 196616 | tf_op jit(solution)/shard_map/ppermute | solution.py:31
  31.5 52.3 %all-to-all-start.3 = ((bf16[8,4,4,16,512]{4,3,2,1,0:T(8,128)(2,1)}), bf16[8,4,4,16,512]{4,3,2,1,0:T(8,128)(2,1)S(1)}, u32[]{:S(2)}, u32[]{:S(2)}) async-start(bf16[8,4,4,16,512]{4,3,2,1,0:T(8,128)(2,1)} %broadcast_in_dim.15), calls=%async_computation.3 | async-start | bytes 4194304 | tf_op jit(solution)/shard_map/all_to_all | solution.py:41
  35.9 6.7 %collective-permute-start.8 = (bf16[8,2,16,512]{3,2,1,0:T(8,128)(2,1)S(1)}, bf16[8,2,16,512]{3,2,1,0:T(8,128)(2,1)S(1)}, u32[]{:S(2)}, u32[]{:S(2)}) collective-permute-start(bf16[8,2,16,512]{3,2,1,0:T(8,128)(2,1)S(1)} %all-to-all-done.w0), channel_id=1, source_target_pairs={{0,2},{1,3},{2,0},{3,1},{4,6},{5,7},{6,4},{7,5},{8,10},{9,11},{10,... | collective-permute-start | bytes 786440 | tf_op jit(solution)/shard_map/ppermute | solution.py:26
  38.1 10.0 %collective-permute-start.7 = (bf16[8,2,16,512]{3,2,1,0:T(8,128)(2,1)S(1)}, bf16[8,2,16,512]{3,2,1,0:T(8,128)(2,1)S(1)}, u32[]{:S(2)}, u32[]{:S(2)}) collective-permute-start(bf16[8,2,16,512]{3,2,1,0:T(8,128)(2,1)S(1)} %all-to-all-done.w0), channel_id=1, source_target_pairs={{0,3},{1,0},{2,1},{3,2},{4,7},{5,4},{6,5},{7,6},{8,11},{9,8},{10,9... | collective-permute-start | bytes 786440 | tf_op jit(solution)/shard_map/ppermute | solution.py:26
  38.9 9.3 %collective-permute-start.6 = (bf16[8,2,16,512]{3,2,1,0:T(8,128)(2,1)S(1)}, bf16[8,2,16,512]{3,2,1,0:T(8,128)(2,1)S(1)}, u32[]{:S(2)}, u32[]{:S(2)}) collective-permute-start(bf16[8,2,16,512]{3,2,1,0:T(8,128)(2,1)S(1)} %all-to-all-done.w0), channel_id=1, source_target_pairs={{0,1},{1,2},{2,3},{3,0},{4,5},{5,6},{6,7},{7,4},{8,9},{9,10},{10,1... | collective-permute-start | bytes 786440 | tf_op jit(solution)/shard_map/ppermute | solution.py:26
  42.7 5.5 %copy-start.5 = (bf16[8,2,16,512]{3,2,1,0:T(8,128)(2,1)}, bf16[8,2,16,512]{3,2,1,0:T(8,128)(2,1)S(1)}, u32[]{:S(2)}) copy-start(bf16[8,2,16,512]{3,2,1,0:T(8,128)(2,1)S(1)} %collective-permute-done.8.w3) | copy-start | bytes 786436
  48.1 0.7 copy-start.6
  48.1 0.8 copy-start.7
  56.6 47.1 %collective-permute-start.11 = (bf16[6,8,16,512]{3,2,1,0:T(8,128)(2,1)}, bf16[6,8,16,512]{3,2,1,0:T(8,128)(2,1)S(1)}, u32[]{:S(2)}, u32[]{:S(2)}) collective-permute-start(bf16[6,8,16,512]{3,2,1,0:T(8,128)(2,1)} %get-tuple-element.20), channel_id=1, source_target_pairs={{0,2},{1,3},{2,0},{3,1},{4,6},{5,7},{6,4},{7,5},{8,10},{9,11},{10,... | collective-permute-start | bytes 2359304 | tf_op jit(solution)/shard_map/ppermute | solution.py:26
  59.5 33.1 %copy-start.9 = (s32[6]{0:T(128)S(1)}, s32[6]{0:T(128)}, u32[]{:S(2)}) copy-start(s32[6]{0:T(128)} %pair_target.1) | copy-start | bytes 76
  67.9 35.8 %collective-permute-start.9 = (bf16[6,8,16,512]{3,2,1,0:T(8,128)(2,1)}, bf16[6,8,16,512]{3,2,1,0:T(8,128)(2,1)}, u32[]{:S(2)}, u32[]{:S(2)}) collective-permute-start(bf16[6,8,16,512]{3,2,1,0:T(8,128)(2,1)} %get-tuple-element.18), channel_id=1, source_target_pairs={{0,1},{1,2},{2,3},{3,0},{4,5},{5,6},{6,7},{7,4},{8,9},{9,10},{10,1... | collective-permute-start | bytes 2359304 | tf_op jit(solution)/shard_map/ppermute | solution.py:26
  69.2 34.5 %collective-permute-start.10 = (bf16[6,8,16,512]{3,2,1,0:T(8,128)(2,1)}, bf16[6,8,16,512]{3,2,1,0:T(8,128)(2,1)}, u32[]{:S(2)}, u32[]{:S(2)}) collective-permute-start(bf16[6,8,16,512]{3,2,1,0:T(8,128)(2,1)} %get-tuple-element.19), channel_id=1, source_target_pairs={{0,3},{1,0},{2,1},{3,2},{4,7},{5,4},{6,5},{7,6},{8,11},{9,8},{10,9... | collective-permute-start | bytes 2359304 | tf_op jit(solution)/shard_map/ppermute | solution.py:26
  83.8 34.2 %copy-start = (bf16[8,4,4,16,512]{4,3,2,1,0:T(8,128)(2,1)}, bf16[8,4,4,16,512]{4,3,2,1,0:T(8,128)(2,1)S(1)}, u32[]{:S(2)}) copy-start(bf16[8,4,4,16,512]{4,3,2,1,0:T(8,128)(2,1)S(1)} %all-to-all-done.3.basis1.rest_4_) | copy-start | bytes 6291460
  84.7 27.8 %all-to-all-start.2 = ((bf16[8,4,16,512]{3,2,1,0:T(8,128)(2,1)}), bf16[8,4,16,512]{3,2,1,0:T(8,128)(2,1)S(1)}, u32[]{:S(2)}, u32[]{:S(2)}) async-start(bf16[8,4,16,512]{3,2,1,0:T(8,128)(2,1)} %broadcast_in_dim.14), calls=%async_computation.2 | async-start | bytes 1048576 | tf_op jit(solution)/shard_map/all_to_all | solution.py:41
  88.8 92.0 %collective-permute-start.26 = (bf16[8,4,4,16,512]{4,3,2,1,0:T(8,128)(2,1)S(1)}, bf16[8,4,4,16,512]{4,3,2,1,0:T(8,128)(2,1)}, u32[]{:S(2)}, u32[]{:S(2)}) collective-permute-start(bf16[8,4,4,16,512]{4,3,2,1,0:T(8,128)(2,1)S(1)} %all-to-all-done.3.basis1.rest_4_), channel_id=1, source_target_pairs={{0,32},{32,0},{64,96},{96,64},{128,160},{160,128},{192,224},{224,1... | collective-permute-start | bytes 6291464 | tf_op jit(solution)/shard_map/ppermute | solution.py:36
  92.6 3.9 %collective-permute-start.2 = (s32[6]{0:T(128)S(1)}, s32[6]{0:T(128)S(1)}, u32[]{:S(2)}, u32[]{:S(2)}) collective-permute-start(s32[6]{0:T(128)S(1)} %copy-done.9), channel_id=1, source_target_pairs={{0,2},{1,3},{2,0},{3,1},{4,6},{5,7},{6,4},{7,5},{8,10},{9,11},{10,... | collective-permute-start | bytes 80 | tf_op jit(solution)/shard_map/ppermute | solution.py:26
  96.5 7.2 %copy-start.10 = (s32[6]{0:T(128)}, s32[6]{0:T(128)S(1)}, u32[]{:S(2)}) copy-start(s32[6]{0:T(128)S(1)} %collective-permute-done.2.t3) | copy-start | bytes 76
  96.5 3.0 %collective-permute-start.1 = (s32[6]{0:T(128)S(1)}, s32[6]{0:T(128)S(1)}, u32[]{:S(2)}, u32[]{:S(2)}) collective-permute-start(s32[6]{0:T(128)S(1)} %copy-done.9), channel_id=1, source_target_pairs={{0,3},{1,0},{2,1},{3,2},{4,7},{5,4},{6,5},{7,6},{8,11},{9,8},{10,9... | collective-permute-start | bytes 80 | tf_op jit(solution)/shard_map/ppermute | solution.py:26
  99.5 4.2 %copy-start.11 = (s32[6]{0:T(128)}, s32[6]{0:T(128)S(1)}, u32[]{:S(2)}) copy-start(s32[6]{0:T(128)S(1)} %collective-permute-done.1.t2) | copy-start | bytes 76
  99.5 4.2 %collective-permute-start = (s32[6]{0:T(128)S(1)}, s32[6]{0:T(128)S(1)}, u32[]{:S(2)}, u32[]{:S(2)}) collective-permute-start(s32[6]{0:T(128)S(1)} %copy-done.9), channel_id=1, source_target_pairs={{0,1},{1,2},{2,3},{3,0},{4,5},{5,6},{6,7},{7,4},{8,9},{9,10},{10,1... | collective-permute-start | bytes 80 | tf_op jit(solution)/shard_map/ppermute | solution.py:26
  103.7 0.5 copy-start.12
  103.7 0.9 copy-start.3
  109.6 5.6 %collective-permute-start.12 = (bf16[8,8,16,512]{3,2,1,0:T(8,128)(2,1)}, bf16[8,8,16,512]{3,2,1,0:T(8,128)(2,1)}, u32[]{:S(2)}, u32[]{:S(2)}) collective-permute-start(bf16[8,8,16,512]{3,2,1,0:T(8,128)(2,1)} %get-tuple-element.22), channel_id=1, source_target_pairs={{0,32},{32,0},{64,96},{96,64},{128,160},{160,128},{192,224},{224,1... | collective-permute-start | bytes 3145736 | tf_op jit(solution)/shard_map/ppermute | solution.py:36
  112.6 61.4 %copy-start.1 = (bf16[8,4,16,512]{3,2,1,0:T(8,128)(2,1)}, bf16[8,4,16,512]{3,2,1,0:T(8,128)(2,1)S(1)}, u32[]{:S(2)}) copy-start(bf16[8,4,16,512]{3,2,1,0:T(8,128)(2,1)S(1)} %all-to-all-done.2.basis0.rest_0_) | copy-start | bytes 1572868
  112.6 14.9 %collective-permute-start.21 = (bf16[8,4,16,512]{3,2,1,0:T(8,128)(2,1)S(1)}, bf16[8,4,16,512]{3,2,1,0:T(8,128)(2,1)S(1)}, u32[]{:S(2)}, u32[]{:S(2)}) collective-permute-start(bf16[8,4,16,512]{3,2,1,0:T(8,128)(2,1)S(1)} %all-to-all-done.2.basis0.rest_0_), channel_id=1, source_target_pairs={{0,128},{32,160},{64,192},{96,224},{128,0},{160,32},{192,64},{224,... | collective-permute-start | bytes 1572872 | tf_op jit(solution)/shard_map/ppermute | solution.py:31
  112.6 23.7 %collective-permute-start.20 = (bf16[8,4,16,512]{3,2,1,0:T(8,128)(2,1)S(1)}, bf16[8,4,16,512]{3,2,1,0:T(8,128)(2,1)}, u32[]{:S(2)}, u32[]{:S(2)}) collective-permute-start(bf16[8,4,16,512]{3,2,1,0:T(8,128)(2,1)S(1)} %all-to-all-done.2.basis0.rest_0_), channel_id=1, source_target_pairs={{0,192},{32,224},{64,0},{96,32},{128,64},{160,96},{192,128},{224,1... | collective-permute-start | bytes 1572872 | tf_op jit(solution)/shard_map/ppermute | solution.py:31
  114.2 25.1 %collective-permute-start.19 = (bf16[8,4,16,512]{3,2,1,0:T(8,128)(2,1)S(1)}, bf16[8,4,16,512]{3,2,1,0:T(8,128)(2,1)}, u32[]{:S(2)}, u32[]{:S(2)}) collective-permute-start(bf16[8,4,16,512]{3,2,1,0:T(8,128)(2,1)S(1)} %all-to-all-done.2.basis0.rest_0_), channel_id=1, source_target_pairs={{0,64},{32,96},{64,128},{96,160},{128,192},{160,224},{192,0},{224,... | collective-permute-start | bytes 1572872 | tf_op jit(solution)/shard_map/ppermute | solution.py:31
  118.0 27.2 %collective-permute-start.13 = (bf16[2,8,16,512]{3,2,1,0:T(8,128)(2,1)}, bf16[2,8,16,512]{3,2,1,0:T(8,128)(2,1)S(1)}, u32[]{:S(2)}, u32[]{:S(2)}) collective-permute-start(bf16[2,8,16,512]{3,2,1,0:T(8,128)(2,1)} %get-tuple-element.24), channel_id=1, source_target_pairs={{0,64},{32,96},{64,128},{96,160},{128,192},{160,224},{192,0},{224,... | collective-permute-start | bytes 786440 | tf_op jit(solution)/shard_map/ppermute | solution.py:31
  127.5 53.3 %copy-start.4 = (bf16[8,4,16,512]{3,2,1,0:T(8,128)(2,1)}, bf16[8,4,16,512]{3,2,1,0:T(8,128)(2,1)S(1)}, u32[]{:S(2)}) copy-start(bf16[8,4,16,512]{3,2,1,0:T(8,128)(2,1)S(1)} %collective-permute-done.21.rest_3_) | copy-start | bytes 1572868
  127.5 18.3 %collective-permute-start.14 = (bf16[2,8,16,512]{3,2,1,0:T(8,128)(2,1)}, bf16[2,8,16,512]{3,2,1,0:T(8,128)(2,1)}, u32[]{:S(2)}, u32[]{:S(2)}) collective-permute-start(bf16[2,8,16,512]{3,2,1,0:T(8,128)(2,1)} %get-tuple-element.25), channel_id=1, source_target_pairs={{0,192},{32,224},{64,0},{96,32},{128,64},{160,96},{192,128},{224,1... | collective-permute-start | bytes 786440 | tf_op jit(solution)/shard_map/ppermute | solution.py:31
  136.2 13.8 %collective-permute-start.15 = (bf16[2,8,16,512]{3,2,1,0:T(8,128)(2,1)}, bf16[2,8,16,512]{3,2,1,0:T(8,128)(2,1)}, u32[]{:S(2)}, u32[]{:S(2)}) collective-permute-start(bf16[2,8,16,512]{3,2,1,0:T(8,128)(2,1)} %get-tuple-element.26), channel_id=1, source_target_pairs={{0,128},{32,160},{64,192},{96,224},{128,0},{160,32},{192,64},{224,... | collective-permute-start | bytes 786440 | tf_op jit(solution)/shard_map/ppermute | solution.py:31
  139.3 41.5 %collective-permute-start.22 = (bf16[8,4,16,512]{3,2,1,0:T(8,128)(2,1)S(1)}, bf16[8,4,16,512]{3,2,1,0:T(8,128)(2,1)}, u32[]{:S(2)}, u32[]{:S(2)}) collective-permute-start(bf16[8,4,16,512]{3,2,1,0:T(8,128)(2,1)S(1)} %all-to-all-done.2.basis0.rest_0_), channel_id=1, source_target_pairs={{0,32},{32,0},{64,96},{96,64},{128,160},{160,128},{192,224},{224,1... | collective-permute-start | bytes 1572872 | tf_op jit(solution)/shard_map/ppermute | solution.py:36
  145.2 5.8 %copy-start.8 = (bf16[2,8,16,512]{3,2,1,0:T(8,128)(2,1)}, bf16[2,8,16,512]{3,2,1,0:T(8,128)(2,1)S(1)}, u32[]{:S(2)}) copy-start(bf16[2,8,16,512]{3,2,1,0:T(8,128)(2,1)S(1)} %collective-permute-done.13.e1) | copy-start | bytes 786436
  145.2 35.6 %collective-permute-start.25 = (bf16[8,4,16,512]{3,2,1,0:T(8,128)(2,1)S(1)}, bf16[8,4,16,512]{3,2,1,0:T(8,128)(2,1)}, u32[]{:S(2)}, u32[]{:S(2)}) collective-permute-start(bf16[8,4,16,512]{3,2,1,0:T(8,128)(2,1)S(1)} %collective-permute-done.21.rest_3_), channel_id=1, source_target_pairs={{0,32},{32,0},{64,96},{96,64},{128,160},{160,128},{192,224},{224,1... | collective-permute-start | bytes 1572872 | tf_op jit(solution)/shard_map/ppermute | solution.py:36
  145.8 35.0 %collective-permute-start.24 = (bf16[8,4,16,512]{3,2,1,0:T(8,128)(2,1)}, bf16[8,4,16,512]{3,2,1,0:T(8,128)(2,1)}, u32[]{:S(2)}, u32[]{:S(2)}) collective-permute-start(bf16[8,4,16,512]{3,2,1,0:T(8,128)(2,1)} %collective-permute-done.20.rest_2_), channel_id=1, source_target_pairs={{0,32},{32,0},{64,96},{96,64},{128,160},{160,128},{192,224},{224,1... | collective-permute-start | bytes 1572872 | tf_op jit(solution)/shard_map/ppermute | solution.py:36
  150.1 30.7 %collective-permute-start.23 = (bf16[8,4,16,512]{3,2,1,0:T(8,128)(2,1)}, bf16[8,4,16,512]{3,2,1,0:T(8,128)(2,1)}, u32[]{:S(2)}, u32[]{:S(2)}) collective-permute-start(bf16[8,4,16,512]{3,2,1,0:T(8,128)(2,1)} %collective-permute-done.19.rest_1_), channel_id=1, source_target_pairs={{0,32},{32,0},{64,96},{96,64},{128,160},{160,128},{192,224},{224,1... | collective-permute-start | bytes 1572872 | tf_op jit(solution)/shard_map/ppermute | solution.py:36

commit v3 on v2

--- a/solution.py
+++ b/solution.py
@@ -147,21 +147,21 @@
     )(dev, pair_source, sector_slot, wm, left, right)
 
 
-def half_kernel(dev, pair_source, sector_slot, basis0, basis1, left, out, ordered):
+def half_kernel(dev, pair_source, sector_slot, bases, left, out, ordered):
     p = pl.program_id(0)
     x, c, _, y = place(dev)
 
     @pl.when(p == 0)
     def _():
         for k in range(NY):
-            ordered[0, :, source_y(y, k)] = basis0[:, k]
-            ordered[1, :, source_y(y, k)] = basis1[:, 0, k]
+            for a in range(SLOTS):
+                ordered[a, :, source_y(y, k)] = bases[:, a, k]
 
     a = sector_slot[pair_source[p]] - (x * NC + c) * SLOTS
     out[0] = jnp.dot(left[0], ordered[a].reshape(K, K), preferred_element_type=F32).astype(BF)
 
 
-def half(dev, pair_source, sector_slot, basis0, basis1, left):
+def half(dev, pair_source, sector_slot, bases, left):
     pair = pl.BlockSpec((1, K, K), lambda p: (p, 0, 0))
     return pl.pallas_call(
         half_kernel,
@@ -169,14 +169,13 @@
         out_shape=jax.ShapeDtypeStruct((PAIRS, K, K), BF),
         in_specs=[SMEM] * 3
         + [
-            pl.BlockSpec((NZ, NY, ROWS, K), lambda p: (0, 0, 0, 0)),
-            pl.BlockSpec((NZ, 1, NY, ROWS, K), lambda p: (0, 0, 0, 0, 0)),
+            pl.BlockSpec((NZ, SLOTS, NY, ROWS, K), lambda p: (0, 0, 0, 0, 0)),
             pair,
         ],
         out_specs=pair,
         scratch_shapes=[pltpu.VMEM((SLOTS, NZ, NY, ROWS, K), BF)],
         name="half",
-    )(dev, pair_source, sector_slot, basis0, basis1, left)
+    )(dev, pair_source, sector_slot, bases, left)
 
 
 def rotate_kernel(dev, pair_target, sector_slot, half_ref, *rest):
@@ -201,17 +200,23 @@
 
             for core in range(NC):
                 mine = tables[core * 5 : core * 5 + 5]
-                for n in range(NX):
+
+                @pl.when((other == core) & (at == 0))
+                def _(table=mine[0]):
+                    for k in range(NY):
+                        copy(table.at[:, a, k], k)
+
+                for n in range(1, NX):
 
                     @pl.when((other == core) & (a == 0) & (at == n))
                     def _(table=mine[n]):
                         for k in range(NY):
                             copy(table.at[:, k], k)
 
-                @pl.when((other == core) & (a == 1))
+                @pl.when((other == core) & (a == 1) & (at > 0))
                 def _(table=mine[4]):
                     for k in range(NY):
-                        copy(table.at[:, at, k], k)
+                        copy(table.at[:, at - 1, k], k)
 
             return carry
 
@@ -350,12 +355,11 @@
 
     w_z = spread_z(wavefunction)
     b_y = [sector_bases] + [shift_y(sector_bases, d) for d in DIST]
-    b_y = jnp.stack(b_y)
+    b_y = jnp.stack(b_y, axis=1)
     b_y, w_z = lax.optimization_barrier((b_y, w_z))
     ws = [w_z] + [shift_y(w_z, d) for d in DIST]
-    b_0 = spread_z(b_y[:, 0])
-    b_1 = b_y[:, 1]
-    b_1 = jnp.stack([b_1] + [shift_x(b_1, d) for d in DIST])
+    b_0 = spread_z(b_y)
+    b_1 = jnp.stack([shift_x(b_y[1], d) for d in DIST])
     b_1 = spread_z(b_1)
     targets = [pair_target] + [shift_y(pair_target, d) for d in DIST]
 
@@ -365,9 +369,10 @@
     near = near_products(dev, pair_source, sector_slot, wm, left, right_env)
     got = [near[0], shift_y(near[1], 1), shift_y(near[2], 3), far]
 
-    tables = [b_0] + [shift_x(b_0, d) for d in DIST] + [b_1]
+    slot_0 = b_0[:, 0]
+    tables = [b_0] + [shift_x(slot_0, d) for d in DIST] + [b_1]
     tables = tables + [swap_core(t) for t in tables]
-    halves = half(dev, pair_source, sector_slot, b_0, b_1, left_env)
+    halves = half(dev, pair_source, sector_slot, b_0, left_env)
 
     mine, other = by_target(dev, sector_slot, targets, got)
     other = swap_core(other)

time: 190 us -> 185 us (0.974)
  blocking collectives: 19.2 us -> 0 us
  starting transfers between devices: 54.1 us -> 63.8 us
  waiting for transfers between devices: 65.9 us -> 70.2 us
    all_to_all x1 -> x0, blocking collectives: 19.2 us -> none  [exchange_z(): lax.all_to_all(tiles, 'op', 0, 0, axis_index_groups=groups, tiled=True)]
    ppermute x12, waiting for transfers between devices: 17.5 us -> 24 us  [shift_y(): return lax.ppermute(a, 'op', perm)]
    all_to_all x3 -> x4, starting transfers between devices: 17.5 us -> 23.5 us  [exchange_z(): lax.all_to_all(tiles, 'op', 0, 0, axis_index_groups=groups, tiled=True)]
    all_to_all x3 -> x4, waiting for transfers between devices: 15.7 us -> 10.8 us  [exchange_z(): lax.all_to_all(tiles, 'op', 0, 0, axis_index_groups=groups, tiled=True)]
    ppermute x9, starting transfers between devices: 8.4 us -> 11.5 us  [shift_x(): return lax.ppermute(a, 'sector', perm)]
  transfers between devices with their start and end apart: 30 -> 31, of which waited for: 18 -> 16; matrix products, arithmetic and copies ran while one was open for 1% -> 1% of each run, Pallas kernels for 18% -> 19%
where the time goes in v3:
time: 185 us; the launch traced here: 184 us
  waiting for transfers between devices  70.2 us (38%)
  starting transfers between devices  63.8 us (34%)
  Pallas kernels  42 us (23%)
  local copies, waits for them, and re-layouts  6.61 us (4%)
    ppermute x9, waiting for transfers between devices, shift_x(): return lax.ppermute(a, 'sector', perm)  32.9 us
    ppermute x12, waiting for transfers between devices, shift_y(): return lax.ppermute(a, 'op', perm)  24 us
    all_to_all x4, starting transfers between devices, exchange_z(): lax.all_to_all(tiles, 'op', 0, 0, axis_index_groups=groups, tiled=True)  23.5 us
    ppermute x12, starting transfers between devices, shift_y(): return lax.ppermute(a, 'op', perm)  19.7 us
    ppermute x9, starting transfers between devices, shift_x(): return lax.ppermute(a, 'sector', perm)  11.5 us
    all_to_all x4, waiting for transfers between devices, exchange_z(): lax.all_to_all(tiles, 'op', 0, 0, axis_index_groups=groups, tiled=True)  10.8 us
    ppermute x6, starting transfers between devices, swap_core(): return lax.ppermute(a, 'sector', perm)  9.16 us
    pallas_call x1, Pallas kernels, near_products(): pl.pallas_call(near_kernel, out_shape=[CHUNK] * 3, grid_spec=pltpu.Prefet...  8.32 us
  transfers between devices with their start and end apart: 31, of which 16 were waited for; matrix products, arithmetic and copies ran while one was open for 1% of the time, Pallas kernels for 19%

profile of v3, /device:TPU:1, one launch (start us, length us, event | category | flops | bytes accessed | tf_op | source)
XLA Modules:
  0.0 184.3 jit_solution(5250035840183449230)
XLA Ops:
  0.6 1.5 broadcast_in_dim.13
  2.1 9.0 %all-to-all-start = ((bf16[8,2,16,512]{3,2,1,0:T(8,128)(2,1)}), bf16[8,2,16,512]{3,2,1,0:T(8,128)(2,1)S(1)}, u32[]{:S(2)}, u32[]{:S(2)}) async-start(bf16[8,2,16,512]{3,2,1,0:T(8,128)(2,1)} %broadcast_in_dim.13), calls=%async_computation | async-start | bytes 524288 | tf_op jit(solution)/shard_map/all_to_all | solution.py:41
  11.1 1.3 collective-permute-start.3
  12.4 2.6 %collective-permute-start.5 = (bf16[2,16,512]{2,1,0:T(8,128)(2,1)}, bf16[2,16,512]{2,1,0:T(8,128)(2,1)S(1)}, u32[]{:S(2)}, u32[]{:S(2)}) collective-permute-start(bf16[2,16,512]{2,1,0:T(8,128)(2,1)} %param.9), channel_id=1, source_target_pairs={{0,2},{1,3},{2,0},{3,1},{4,6},{5,7},{6,4},{7,5},{8,10},{9,11},{10,... | collective-permute-start | bytes 98312 | tf_op jit(solution)/shard_map/ppermute | solution.py:26
  15.0 1.1 collective-permute-start.4
  16.1 0.9 collective-permute-done.5
  17.0 1.3 collective-permute-done.4
  19.1 2.5 %all-to-all-done.w0 = bf16[8,2,16,512]{3,2,1,0:T(8,128)(2,1)S(1)} async-done(((bf16[8,2,16,512]{3,2,1,0:T(8,128)(2,1)}), bf16[8,2,16,512]{3,2,1,0:T(8,128)(2,1)S(1)}, u32[]{:S(2)}, u32[]{:S(2)}) %all-to-all-start) | async-done | bytes 262176 | tf_op jit(solution)/shard_map/all_to_all | solution.py:41
  21.6 2.8 %collective-permute-start.21 = (bf16[4,16,512]{2,1,0:T(8,128)(2,1)S(1)}, bf16[4,16,512]{2,1,0:T(8,128)(2,1)S(1)}, u32[]{:S(2)}, u32[]{:S(2)}) collective-permute-start(bf16[4,16,512]{2,1,0:T(8,128)(2,1)S(1)} %slice_bitcast_fusion.1), channel_id=1, source_target_pairs={{0,128},{32,160},{64,192},{96,224},{128,0},{160,32},{192,64},{224,... | collective-permute-start | bytes 196616 | tf_op jit(solution)/shard_map/ppermute | solution.py:31
  24.5 0.9 collective-permute-start.20
  26.3 1.2 collective-permute-done.20
  27.6 2.3 %collective-permute-done.19 = bf16[4,16,512]{2,1,0:T(8,128)(2,1)S(1)} collective-permute-done((bf16[4,16,512]{2,1,0:T(8,128)(2,1)S(1)}, bf16[4,16,512]{2,1,0:T(8,128)(2,1)S(1)}, u32[]{:S(2)}, u32[]{:S(2)}) %collective-permute-start.19) | collective-permute-done | bytes 65568 | tf_op jit(solution)/shard_map/ppermute | solution.py:31
  29.9 1.3 broadcast_in_dim.15
  31.2 4.5 %all-to-all-start.3 = ((bf16[8,3,4,16,512]{4,3,2,1,0:T(8,128)(2,1)}), bf16[8,3,4,16,512]{4,3,2,1,0:T(8,128)(2,1)S(1)}, u32[]{:S(2)}, u32[]{:S(2)}) async-start(bf16[8,3,4,16,512]{4,3,2,1,0:T(8,128)(2,1)} %broadcast_in_dim.15), calls=%async_computation.3 | async-start | bytes 3145728 | tf_op jit(solution)/shard_map/all_to_all | solution.py:41
  35.7 2.1 %collective-permute-start.8 = (bf16[8,2,16,512]{3,2,1,0:T(8,128)(2,1)S(1)}, bf16[8,2,16,512]{3,2,1,0:T(8,128)(2,1)S(1)}, u32[]{:S(2)}, u32[]{:S(2)}) collective-permute-start(bf16[8,2,16,512]{3,2,1,0:T(8,128)(2,1)S(1)} %all-to-all-done.w0), channel_id=1, source_target_pairs={{0,2},{1,3},{2,0},{3,1},{4,6},{5,7},{6,4},{7,5},{8,10},{9,11},{10,... | collective-permute-start | bytes 786440 | tf_op jit(solution)/shard_map/ppermute | solution.py:26
  39.3 3.1 %collective-permute-done.8.w3 = bf16[8,2,16,512]{3,2,1,0:T(8,128)(2,1)S(1)} collective-permute-done((bf16[8,2,16,512]{3,2,1,0:T(8,128)(2,1)S(1)}, bf16[8,2,16,512]{3,2,1,0:T(8,128)(2,1)S(1)}, u32[]{:S(2)}, u32[]{:S(2)}) %collective-permute-start.8) | collective-permute-done | bytes 262176 | tf_op jit(solution)/shard_map/ppermute | solution.py:26
  42.4 5.5 %collective-permute-done.7.w2 = bf16[8,2,16,512]{3,2,1,0:T(8,128)(2,1)S(1)} collective-permute-done((bf16[8,2,16,512]{3,2,1,0:T(8,128)(2,1)S(1)}, bf16[8,2,16,512]{3,2,1,0:T(8,128)(2,1)S(1)}, u32[]{:S(2)}, u32[]{:S(2)}) %collective-permute-start.7) | collective-permute-done | bytes 262176 | tf_op jit(solution)/shard_map/ppermute | solution.py:26
  48.7 7.6 %far_products.1 = (bf16[6,8,16,512]{3,2,1,0:T(8,128)(2,1)}, bf16[2,8,4,16,512]{4,3,2,1,0:T(8,128)(2,1)}) custom-call(s32[1]{0:T(128)} %bitcast.dev, s32[6]{0:T(128)} %pair_source.5, s32[16]{0:T(128)} %sector_slot.11, s32[16]{0:T(128)} %orders.3, bf16[8,2,16,512]{3,2,1,0:T(8,128)(2,1)} %copy-done.2, bf16[8,2,16,512]{3,2,1,0:T(8,128)(2,1)} %copy-done.8, ...), custom_call_target="tpu_custom_call" | custom-call | tf_op jit(solution)/shard_map/far_products/pallas_call | solution.py:119
  56.3 2.8 %collective-permute-start.11 = (bf16[6,8,16,512]{3,2,1,0:T(8,128)(2,1)}, bf16[6,8,16,512]{3,2,1,0:T(8,128)(2,1)S(1)}, u32[]{:S(2)}, u32[]{:S(2)}) collective-permute-start(bf16[6,8,16,512]{3,2,1,0:T(8,128)(2,1)} %get-tuple-element.20), channel_id=1, source_target_pairs={{0,2},{1,3},{2,0},{3,1},{4,6},{5,7},{6,4},{7,5},{8,10},{9,11},{10,... | collective-permute-start | bytes 2359304 | tf_op jit(solution)/shard_map/ppermute | solution.py:26
  59.2 8.3 %near_products.1 = (bf16[6,8,16,512]{3,2,1,0:T(8,128)(2,1)}, bf16[6,8,16,512]{3,2,1,0:T(8,128)(2,1)}, bf16[6,8,16,512]{3,2,1,0:T(8,128)(2,1)}) custom-call(s32[1]{0:T(128)} %bitcast.dev, s32[6]{0:T(128)} %pair_source.5, s32[16]{0:T(128)} %sector_slot.11, bf16[2,8,4,16,512]{4,3,2,1,0:T(8,128)(2,1)} %get-tuple-element.16.wm, ...), custom_call_target="tpu_custom_call" | custom-call | tf_op jit(solution)/shard_map/near_products/pallas_call | solution.py:133
  67.5 1.3 collective-permute-start.9
  68.8 1.4 collective-permute-start.10
  70.2 2.7 %all-to-all-done.3.rest_4_ = bf16[8,3,4,16,512]{4,3,2,1,0:T(8,128)(2,1)S(1)} async-done(((bf16[8,3,4,16,512]{4,3,2,1,0:T(8,128)(2,1)}), bf16[8,3,4,16,512]{4,3,2,1,0:T(8,128)(2,1)S(1)}, u32[]{:S(2)}, u32[]{:S(2)}) %all-to-all-start.3) | async-done | bytes 1572896 | tf_op jit(solution)/shard_map/all_to_all | solution.py:41
  72.9 1.3 broadcast_in_dim.14
  74.2 3.6 %all-to-all-start.2 = ((bf16[8,2,4,16,512]{4,3,2,1,0:T(8,128)(2,1)}), bf16[8,2,4,16,512]{4,3,2,1,0:T(8,128)(2,1)S(1)}, u32[]{:S(2)}, u32[]{:S(2)}) async-start(bf16[8,2,4,16,512]{4,3,2,1,0:T(8,128)(2,1)} %broadcast_in_dim.14), calls=%async_computation.2 | async-start | bytes 2097152 | tf_op jit(solution)/shard_map/all_to_all | solution.py:41
  77.8 2.3 %collective-permute-start.2 = (s32[6]{0:T(128)S(1)}, s32[6]{0:T(128)S(1)}, u32[]{:S(2)}, u32[]{:S(2)}) collective-permute-start(s32[6]{0:T(128)S(1)} %copy-done.10), channel_id=1, source_target_pairs={{0,2},{1,3},{2,0},{3,1},{4,6},{5,7},{6,4},{7,5},{8,10},{9,11},{10,... | collective-permute-start | bytes 80 | tf_op jit(solution)/shard_map/ppermute | solution.py:26
  80.9 9.6 %collective-permute-done.2.t3 = s32[6]{0:T(128)S(1)} collective-permute-done((s32[6]{0:T(128)S(1)}, s32[6]{0:T(128)S(1)}, u32[]{:S(2)}, u32[]{:S(2)}) %collective-permute-start.2) | collective-permute-done | bytes 56 | tf_op jit(solution)/shard_map/ppermute | solution.py:26
  90.5 2.5 %collective-permute-start = (s32[6]{0:T(128)S(1)}, s32[6]{0:T(128)S(1)}, u32[]{:S(2)}, u32[]{:S(2)}) collective-permute-start(s32[6]{0:T(128)S(1)} %copy-done.10), channel_id=1, source_target_pairs={{0,1},{1,2},{2,3},{3,0},{4,5},{5,6},{6,7},{7,4},{8,9},{9,10},{10,1... | collective-permute-start | bytes 80 | tf_op jit(solution)/shard_map/ppermute | solution.py:26
  92.9 1.7 collective-permute-done.1.t2
  94.6 1.9 %collective-permute-done.t1 = s32[6]{0:T(128)S(1)} collective-permute-done((s32[6]{0:T(128)S(1)}, s32[6]{0:T(128)S(1)}, u32[]{:S(2)}, u32[]{:S(2)}) %collective-permute-start) | collective-permute-done | bytes 56 | tf_op jit(solution)/shard_map/ppermute | solution.py:26
  97.5 4.9 %by_target.1 = (f32[8,8,16,512]{3,2,1,0:T(8,128)}, bf16[8,8,16,512]{3,2,1,0:T(8,128)(2,1)}) custom-call(s32[1]{0:T(128)} %bitcast.dev, s32[16]{0:T(128)} %sector_slot.11, s32[6]{0:T(128)} %pair_target.1, s32[6]{0:T(128)} %copy-done.13, s32[6]{0:T(128)} %copy-done.12, s32[6]{0:T(128)} %copy-done.11, bf16[6,8,16,512]{3,2,1,0:T(8,128)(2,1)} %get-tuple-element.17.g0, ...), custom_call_target="tpu_custom_call" | custom-call | tf_op jit(solution)/shard_map/by_target/pallas_call | solution.py:267
  102.4 3.8 %collective-permute-start.12 = (bf16[8,8,16,512]{3,2,1,0:T(8,128)(2,1)}, bf16[8,8,16,512]{3,2,1,0:T(8,128)(2,1)}, u32[]{:S(2)}, u32[]{:S(2)}) collective-permute-start(bf16[8,8,16,512]{3,2,1,0:T(8,128)(2,1)} %get-tuple-element.22), channel_id=1, source_target_pairs={{0,32},{32,0},{64,96},{96,64},{128,160},{160,128},{192,224},{224,1... | collective-permute-start | bytes 3145736 | tf_op jit(solution)/shard_map/ppermute | solution.py:36
  106.3 2.5 %collective-permute-done.12.other = bf16[8,8,16,512]{3,2,1,0:T(8,128)(2,1)} collective-permute-done((bf16[8,8,16,512]{3,2,1,0:T(8,128)(2,1)}, bf16[8,8,16,512]{3,2,1,0:T(8,128)(2,1)}, u32[]{:S(2)}, u32[]{:S(2)}) %collective-permute-start.12) | collective-permute-done | bytes 1048608 | tf_op jit(solution)/shard_map/ppermute | solution.py:36
  108.8 2.8 %over_cores.1 = (f32[2,8,16,512]{3,2,1,0:T(8,128)}, bf16[2,8,16,512]{3,2,1,0:T(8,128)(2,1)}, bf16[2,8,16,512]{3,2,1,0:T(8,128)(2,1)}, bf16[2,8,16,512]{3,2,1,0:T(8,128)(2,1)}) custom-call(s32[1]{0:T(128)} %bitcast.dev, f32[8,8,16,512]{3,2,1,0:T(8,128)} %get-tuple-element.21.mine, bf16[8,8,16,512]{3,2,1,0:T(8,128)(2,1)} %collective-permute-done.12.other), custom_call_target="tpu_custom_call" | custom-call | tf_op jit(solution)/shard_map/over_cores/pallas_call | solution.py:295
  111.7 2.7 %collective-permute-start.14 = (bf16[2,8,16,512]{3,2,1,0:T(8,128)(2,1)}, bf16[2,8,16,512]{3,2,1,0:T(8,128)(2,1)}, u32[]{:S(2)}, u32[]{:S(2)}) collective-permute-start(bf16[2,8,16,512]{3,2,1,0:T(8,128)(2,1)} %get-tuple-element.25), channel_id=1, source_target_pairs={{0,192},{32,224},{64,0},{96,32},{128,64},{160,96},{192,128},{224,1... | collective-permute-start | bytes 786440 | tf_op jit(solution)/shard_map/ppermute | solution.py:31
  114.4 3.0 %collective-permute-start.18 = (bf16[8,4,16,512]{3,2,1,0:T(8,128)(2,1)S(1)}, bf16[8,4,16,512]{3,2,1,0:T(8,128)(2,1)S(1)}, u32[]{:S(2)}, u32[]{:S(2)}) collective-permute-start(bf16[8,4,16,512]{3,2,1,0:T(8,128)(2,1)S(1)} %slice_bitcast_fusion), channel_id=1, source_target_pairs={{0,128},{32,160},{64,192},{96,224},{128,0},{160,32},{192,64},{224,... | collective-permute-start | bytes 1572872 | tf_op jit(solution)/shard_map/ppermute | solution.py:31
  117.5 20.0 %collective-permute-done.13.e1 = bf16[2,8,16,512]{3,2,1,0:T(8,128)(2,1)S(1)} collective-permute-done((bf16[2,8,16,512]{3,2,1,0:T(8,128)(2,1)}, bf16[2,8,16,512]{3,2,1,0:T(8,128)(2,1)S(1)}, u32[]{:S(2)}, u32[]{:S(2)}) %collective-permute-start.13) | collective-permute-done | bytes 262176 | tf_op jit(solution)/shard_map/ppermute | solution.py:31
  137.4 1.5 collective-permute-start.16
  138.9 1.8 collective-permute-start.22
  140.8 9.0 %collective-permute-done.17.rest_2_ = bf16[8,4,16,512]{3,2,1,0:T(8,128)(2,1)} collective-permute-done((bf16[8,4,16,512]{3,2,1,0:T(8,128)(2,1)S(1)}, bf16[8,4,16,512]{3,2,1,0:T(8,128)(2,1)}, u32[]{:S(2)}, u32[]{:S(2)}) %collective-permute-start.17) | collective-permute-done | bytes 524320 | tf_op jit(solution)/shard_map/ppermute | solution.py:31
  149.8 2.1 %collective-permute-start.24 = (bf16[8,4,16,512]{3,2,1,0:T(8,128)(2,1)}, bf16[8,4,16,512]{3,2,1,0:T(8,128)(2,1)}, u32[]{:S(2)}, u32[]{:S(2)}) collective-permute-start(bf16[8,4,16,512]{3,2,1,0:T(8,128)(2,1)} %collective-permute-done.17.rest_2_), channel_id=1, source_target_pairs={{0,32},{32,0},{64,96},{96,64},{128,160},{160,128},{192,224},{224,1... | collective-permute-start | bytes 1572872 | tf_op jit(solution)/shard_map/ppermute | solution.py:36
  151.9 1.3 collective-permute-start.23
  153.2 2.1 %over_x.1 = bf16[8,2,16,512]{3,2,1,0:T(8,128)(2,1)} custom-call(f32[2,8,16,512]{3,2,1,0:T(8,128)} %get-tuple-element.23.e0, bf16[2,8,16,512]{3,2,1,0:T(8,128)(2,1)} %copy-done.9, bf16[2,8,16,512]{3,2,1,0:T(8,128)(2,1)} %collective-permute-done.14.e2, bf16[2,8,16,512]{3,2,1,0:T(8,128)(2,1)} %collective-permute-done.15.e3), custom_call_target="tpu_custom_call" | custom-call | tf_op jit(solution)/shard_map/over_x/pallas_call | solution.py:313
  155.3 6.4 %all-to-all-start.1 = ((bf16[8,2,16,512]{3,2,1,0:T(8,128)(2,1)}), bf16[8,2,16,512]{3,2,1,0:T(8,128)(2,1)S(1)}, u32[]{:S(2)}, u32[]{:S(2)}) async-start(bf16[8,2,16,512]{3,2,1,0:T(8,128)(2,1)} %over_x.1), calls=%async_computation.1 | async-start | bytes 524288 | tf_op jit(solution)/shard_map/all_to_all | solution.py:41
  161.7 6.8 %half.1.half_ref = bf16[6,512,512]{2,1,0:T(8,128)(2,1)} custom-call(s32[1]{0:T(128)} %bitcast.dev, s32[6]{0:T(128)} %pair_source.5, s32[16]{0:T(128)} %sector_slot.11, bf16[8,2,4,16,512]{4,3,2,1,0:T(8,128)(2,1)} %copy-done, bf16[6,512,512]{2,1,0:T(8,128)(2,1)} %left.1), custom_call_target="tpu_custom_call" | custom-call | tf_op jit(solution)/shard_map/half/pallas_call | solution.py:166
  168.6 5.5 %all-to-all-done.1.parts = bf16[8,2,16,512]{3,2,1,0:T(8,128)(2,1)S(1)} async-done(((bf16[8,2,16,512]{3,2,1,0:T(8,128)(2,1)}), bf16[8,2,16,512]{3,2,1,0:T(8,128)(2,1)S(1)}, u32[]{:S(2)}, u32[]{:S(2)}) %all-to-all-start.1) | async-done | bytes 262176 | tf_op jit(solution)/shard_map/all_to_all | solution.py:41
  174.8 1.6 over_z.1
  176.4 7.7 %rotate.1 = bf16[6,512,512]{2,1,0:T(8,128)(2,1)} custom-call(s32[1]{0:T(128)} %bitcast.dev, s32[6]{0:T(128)} %pair_target.1, s32[16]{0:T(128)} %sector_slot.11, bf16[6,512,512]{2,1,0:T(8,128)(2,1)} %half.1.half_ref, bf16[8,2,4,16,512]{4,3,2,1,0:T(8,128)(2,1)} %copy-done, bf16[8,4,16,512]{3,2,1,0:T(8,128)(2,1)} %collective-permute-done.16.rest_1_, ...), custom_call_target="tpu_custom_call" | custom-call | tf_op jit(solution)/shard_map/rotate/pallas_call | solution.py:234
  (58 shorter events, 6.8 us)
Async XLA Ops:
  2.1 19.5 %all-to-all-start = ((bf16[8,2,16,512]{3,2,1,0:T(8,128)(2,1)}), bf16[8,2,16,512]{3,2,1,0:T(8,128)(2,1)S(1)}, u32[]{:S(2)}, u32[]{:S(2)}) async-start(bf16[8,2,16,512]{3,2,1,0:T(8,128)(2,1)} %broadcast_in_dim.13), calls=%async_computation | async-start | bytes 524288 | tf_op jit(solution)/shard_map/all_to_all | solution.py:41
  11.1 5.0 %collective-permute-start.3 = (bf16[2,16,512]{2,1,0:T(8,128)(2,1)}, bf16[2,16,512]{2,1,0:T(8,128)(2,1)S(1)}, u32[]{:S(2)}, u32[]{:S(2)}) collective-permute-start(bf16[2,16,512]{2,1,0:T(8,128)(2,1)} %param.9), channel_id=1, source_target_pairs={{0,1},{1,2},{2,3},{3,0},{4,5},{5,6},{6,7},{7,4},{8,9},{9,10},{10,1... | collective-permute-start | bytes 98312 | tf_op jit(solution)/shard_map/ppermute | solution.py:26
  12.4 4.6 %collective-permute-start.5 = (bf16[2,16,512]{2,1,0:T(8,128)(2,1)}, bf16[2,16,512]{2,1,0:T(8,128)(2,1)S(1)}, u32[]{:S(2)}, u32[]{:S(2)}) collective-permute-start(bf16[2,16,512]{2,1,0:T(8,128)(2,1)} %param.9), channel_id=1, source_target_pairs={{0,2},{1,3},{2,0},{3,1},{4,6},{5,7},{6,4},{7,5},{8,10},{9,11},{10,... | collective-permute-start | bytes 98312 | tf_op jit(solution)/shard_map/ppermute | solution.py:26
  15.0 3.3 %collective-permute-start.4 = (bf16[2,16,512]{2,1,0:T(8,128)(2,1)}, bf16[2,16,512]{2,1,0:T(8,128)(2,1)S(1)}, u32[]{:S(2)}, u32[]{:S(2)}) collective-permute-start(bf16[2,16,512]{2,1,0:T(8,128)(2,1)} %param.9), channel_id=1, source_target_pairs={{0,3},{1,0},{2,1},{3,2},{4,7},{5,4},{6,5},{7,6},{8,11},{9,8},{10,9... | collective-permute-start | bytes 98312 | tf_op jit(solution)/shard_map/ppermute | solution.py:26
  21.6 26.3 %copy-start.2 = (bf16[8,2,16,512]{3,2,1,0:T(8,128)(2,1)}, bf16[8,2,16,512]{3,2,1,0:T(8,128)(2,1)S(1)}, u32[]{:S(2)}) copy-start(bf16[8,2,16,512]{3,2,1,0:T(8,128)(2,1)S(1)} %all-to-all-done.w0) | copy-start | bytes 786436
  21.6 4.7 %collective-permute-start.21 = (bf16[4,16,512]{2,1,0:T(8,128)(2,1)S(1)}, bf16[4,16,512]{2,1,0:T(8,128)(2,1)S(1)}, u32[]{:S(2)}, u32[]{:S(2)}) collective-permute-start(bf16[4,16,512]{2,1,0:T(8,128)(2,1)S(1)} %slice_bitcast_fusion.1), channel_id=1, source_target_pairs={{0,128},{32,160},{64,192},{96,224},{128,0},{160,32},{192,64},{224,... | collective-permute-start | bytes 196616 | tf_op jit(solution)/shard_map/ppermute | solution.py:31
  24.5 3.1 %collective-permute-start.20 = (bf16[4,16,512]{2,1,0:T(8,128)(2,1)S(1)}, bf16[4,16,512]{2,1,0:T(8,128)(2,1)S(1)}, u32[]{:S(2)}, u32[]{:S(2)}) collective-permute-start(bf16[4,16,512]{2,1,0:T(8,128)(2,1)S(1)} %slice_bitcast_fusion.1), channel_id=1, source_target_pairs={{0,192},{32,224},{64,0},{96,32},{128,64},{160,96},{192,128},{224,1... | collective-permute-start | bytes 196616 | tf_op jit(solution)/shard_map/ppermute | solution.py:31
  25.3 4.5 %collective-permute-start.19 = (bf16[4,16,512]{2,1,0:T(8,128)(2,1)S(1)}, bf16[4,16,512]{2,1,0:T(8,128)(2,1)S(1)}, u32[]{:S(2)}, u32[]{:S(2)}) collective-permute-start(bf16[4,16,512]{2,1,0:T(8,128)(2,1)S(1)} %slice_bitcast_fusion.1), channel_id=1, source_target_pairs={{0,64},{32,96},{64,128},{96,160},{128,192},{160,224},{192,0},{224,... | collective-permute-start | bytes 196616 | tf_op jit(solution)/shard_map/ppermute | solution.py:31
  31.2 41.7 %all-to-all-start.3 = ((bf16[8,3,4,16,512]{4,3,2,1,0:T(8,128)(2,1)}), bf16[8,3,4,16,512]{4,3,2,1,0:T(8,128)(2,1)S(1)}, u32[]{:S(2)}, u32[]{:S(2)}) async-start(bf16[8,3,4,16,512]{4,3,2,1,0:T(8,128)(2,1)} %broadcast_in_dim.15), calls=%async_computation.3 | async-start | bytes 3145728 | tf_op jit(solution)/shard_map/all_to_all | solution.py:41
  35.7 6.7 %collective-permute-start.8 = (bf16[8,2,16,512]{3,2,1,0:T(8,128)(2,1)S(1)}, bf16[8,2,16,512]{3,2,1,0:T(8,128)(2,1)S(1)}, u32[]{:S(2)}, u32[]{:S(2)}) collective-permute-start(bf16[8,2,16,512]{3,2,1,0:T(8,128)(2,1)S(1)} %all-to-all-done.w0), channel_id=1, source_target_pairs={{0,2},{1,3},{2,0},{3,1},{4,6},{5,7},{6,4},{7,5},{8,10},{9,11},{10,... | collective-permute-start | bytes 786440 | tf_op jit(solution)/shard_map/ppermute | solution.py:26
  37.8 10.1 %collective-permute-start.7 = (bf16[8,2,16,512]{3,2,1,0:T(8,128)(2,1)S(1)}, bf16[8,2,16,512]{3,2,1,0:T(8,128)(2,1)S(1)}, u32[]{:S(2)}, u32[]{:S(2)}) collective-permute-start(bf16[8,2,16,512]{3,2,1,0:T(8,128)(2,1)S(1)} %all-to-all-done.w0), channel_id=1, source_target_pairs={{0,3},{1,0},{2,1},{3,2},{4,7},{5,4},{6,5},{7,6},{8,11},{9,8},{10,9... | collective-permute-start | bytes 786440 | tf_op jit(solution)/shard_map/ppermute | solution.py:26
  38.6 9.3 %collective-permute-start.6 = (bf16[8,2,16,512]{3,2,1,0:T(8,128)(2,1)S(1)}, bf16[8,2,16,512]{3,2,1,0:T(8,128)(2,1)S(1)}, u32[]{:S(2)}, u32[]{:S(2)}) collective-permute-start(bf16[8,2,16,512]{3,2,1,0:T(8,128)(2,1)S(1)} %all-to-all-done.w0), channel_id=1, source_target_pairs={{0,1},{1,2},{2,3},{3,0},{4,5},{5,6},{6,7},{7,4},{8,9},{9,10},{10,1... | collective-permute-start | bytes 786440 | tf_op jit(solution)/shard_map/ppermute | solution.py:26
  42.4 5.5 %copy-start.6 = (bf16[8,2,16,512]{3,2,1,0:T(8,128)(2,1)}, bf16[8,2,16,512]{3,2,1,0:T(8,128)(2,1)S(1)}, u32[]{:S(2)}) copy-start(bf16[8,2,16,512]{3,2,1,0:T(8,128)(2,1)S(1)} %collective-permute-done.8.w3) | copy-start | bytes 786436
  47.9 0.7 copy-start.7
  47.9 0.8 copy-start.8
  56.3 40.2 %collective-permute-start.11 = (bf16[6,8,16,512]{3,2,1,0:T(8,128)(2,1)}, bf16[6,8,16,512]{3,2,1,0:T(8,128)(2,1)S(1)}, u32[]{:S(2)}, u32[]{:S(2)}) collective-permute-start(bf16[6,8,16,512]{3,2,1,0:T(8,128)(2,1)} %get-tuple-element.20), channel_id=1, source_target_pairs={{0,2},{1,3},{2,0},{3,1},{4,6},{5,7},{6,4},{7,5},{8,10},{9,11},{10,... | collective-permute-start | bytes 2359304 | tf_op jit(solution)/shard_map/ppermute | solution.py:26
  67.5 10.3 %copy-start.10 = (s32[6]{0:T(128)S(1)}, s32[6]{0:T(128)}, u32[]{:S(2)}) copy-start(s32[6]{0:T(128)} %pair_target.1) | copy-start | bytes 76
  67.5 29.0 %collective-permute-start.9 = (bf16[6,8,16,512]{3,2,1,0:T(8,128)(2,1)}, bf16[6,8,16,512]{3,2,1,0:T(8,128)(2,1)}, u32[]{:S(2)}, u32[]{:S(2)}) collective-permute-start(bf16[6,8,16,512]{3,2,1,0:T(8,128)(2,1)} %get-tuple-element.18), channel_id=1, source_target_pairs={{0,1},{1,2},{2,3},{3,0},{4,5},{5,6},{6,7},{7,4},{8,9},{9,10},{10,1... | collective-permute-start | bytes 2359304 | tf_op jit(solution)/shard_map/ppermute | solution.py:26
  68.8 27.7 %collective-permute-start.10 = (bf16[6,8,16,512]{3,2,1,0:T(8,128)(2,1)}, bf16[6,8,16,512]{3,2,1,0:T(8,128)(2,1)}, u32[]{:S(2)}, u32[]{:S(2)}) collective-permute-start(bf16[6,8,16,512]{3,2,1,0:T(8,128)(2,1)} %get-tuple-element.19), channel_id=1, source_target_pairs={{0,3},{1,0},{2,1},{3,2},{4,7},{5,4},{6,5},{7,6},{8,11},{9,8},{10,9... | collective-permute-start | bytes 2359304 | tf_op jit(solution)/shard_map/ppermute | solution.py:26
  72.9 33.3 %copy-start.1 = (bf16[8,3,4,16,512]{4,3,2,1,0:T(8,128)(2,1)}, bf16[8,3,4,16,512]{4,3,2,1,0:T(8,128)(2,1)S(1)}, u32[]{:S(2)}) copy-start(bf16[8,3,4,16,512]{4,3,2,1,0:T(8,128)(2,1)S(1)} %all-to-all-done.3.rest_4_) | copy-start | bytes 4718596
  74.2 40.2 %all-to-all-start.2 = ((bf16[8,2,4,16,512]{4,3,2,1,0:T(8,128)(2,1)}), bf16[8,2,4,16,512]{4,3,2,1,0:T(8,128)(2,1)S(1)}, u32[]{:S(2)}, u32[]{:S(2)}) async-start(bf16[8,2,4,16,512]{4,3,2,1,0:T(8,128)(2,1)} %broadcast_in_dim.14), calls=%async_computation.2 | async-start | bytes 2097152 | tf_op jit(solution)/shard_map/all_to_all | solution.py:41
  77.8 12.7 %collective-permute-start.2 = (s32[6]{0:T(128)S(1)}, s32[6]{0:T(128)S(1)}, u32[]{:S(2)}, u32[]{:S(2)}) collective-permute-start(s32[6]{0:T(128)S(1)} %copy-done.10), channel_id=1, source_target_pairs={{0,2},{1,3},{2,0},{3,1},{4,6},{5,7},{6,4},{7,5},{8,10},{9,11},{10,... | collective-permute-start | bytes 80 | tf_op jit(solution)/shard_map/ppermute | solution.py:26
  80.1 14.5 %collective-permute-start.1 = (s32[6]{0:T(128)S(1)}, s32[6]{0:T(128)S(1)}, u32[]{:S(2)}, u32[]{:S(2)}) collective-permute-start(s32[6]{0:T(128)S(1)} %copy-done.10), channel_id=1, source_target_pairs={{0,3},{1,0},{2,1},{3,2},{4,7},{5,4},{6,5},{7,6},{8,11},{9,8},{10,9... | collective-permute-start | bytes 80 | tf_op jit(solution)/shard_map/ppermute | solution.py:26
  90.4 6.1 %copy-start.11 = (s32[6]{0:T(128)}, s32[6]{0:T(128)S(1)}, u32[]{:S(2)}) copy-start(s32[6]{0:T(128)S(1)} %collective-permute-done.2.t3) | copy-start | bytes 76
  90.5 6.1 %collective-permute-start = (s32[6]{0:T(128)S(1)}, s32[6]{0:T(128)S(1)}, u32[]{:S(2)}, u32[]{:S(2)}) collective-permute-start(s32[6]{0:T(128)S(1)} %copy-done.10), channel_id=1, source_target_pairs={{0,1},{1,2},{2,3},{3,0},{4,5},{5,6},{6,7},{7,4},{8,9},{9,10},{10,1... | collective-permute-start | bytes 80 | tf_op jit(solution)/shard_map/ppermute | solution.py:26
  94.6 1.9 %copy-start.12 = (s32[6]{0:T(128)}, s32[6]{0:T(128)S(1)}, u32[]{:S(2)}) copy-start(s32[6]{0:T(128)S(1)} %collective-permute-done.1.t2) | copy-start | bytes 76
  96.5 0.5 copy-start.13
  96.5 1.0 copy-start.4
  102.4 6.4 %collective-permute-start.12 = (bf16[8,8,16,512]{3,2,1,0:T(8,128)(2,1)}, bf16[8,8,16,512]{3,2,1,0:T(8,128)(2,1)}, u32[]{:S(2)}, u32[]{:S(2)}) collective-permute-start(bf16[8,8,16,512]{3,2,1,0:T(8,128)(2,1)} %get-tuple-element.22), channel_id=1, source_target_pairs={{0,32},{32,0},{64,96},{96,64},{128,160},{160,128},{192,224},{224,1... | collective-permute-start | bytes 3145736 | tf_op jit(solution)/shard_map/ppermute | solution.py:36
  106.2 70.2 %collective-permute-start.26 = (bf16[8,3,4,16,512]{4,3,2,1,0:T(8,128)(2,1)S(1)}, bf16[8,3,4,16,512]{4,3,2,1,0:T(8,128)(2,1)}, u32[]{:S(2)}, u32[]{:S(2)}) collective-permute-start(bf16[8,3,4,16,512]{4,3,2,1,0:T(8,128)(2,1)S(1)} %all-to-all-done.3.rest_4_), channel_id=1, source_target_pairs={{0,32},{32,0},{64,96},{96,64},{128,160},{160,128},{192,224},{224,1... | collective-permute-start | bytes 4718600 | tf_op jit(solution)/shard_map/ppermute | solution.py:36
  111.7 25.8 %collective-permute-start.13 = (bf16[2,8,16,512]{3,2,1,0:T(8,128)(2,1)}, bf16[2,8,16,512]{3,2,1,0:T(8,128)(2,1)S(1)}, u32[]{:S(2)}, u32[]{:S(2)}) collective-permute-start(bf16[2,8,16,512]{3,2,1,0:T(8,128)(2,1)} %get-tuple-element.24), channel_id=1, source_target_pairs={{0,64},{32,96},{64,128},{96,160},{128,192},{160,224},{192,0},{224,... | collective-permute-start | bytes 786440 | tf_op jit(solution)/shard_map/ppermute | solution.py:31
  111.7 25.8 %collective-permute-start.14 = (bf16[2,8,16,512]{3,2,1,0:T(8,128)(2,1)}, bf16[2,8,16,512]{3,2,1,0:T(8,128)(2,1)}, u32[]{:S(2)}, u32[]{:S(2)}) collective-permute-start(bf16[2,8,16,512]{3,2,1,0:T(8,128)(2,1)} %get-tuple-element.25), channel_id=1, source_target_pairs={{0,192},{32,224},{64,0},{96,32},{128,64},{160,96},{192,128},{224,1... | collective-permute-start | bytes 786440 | tf_op jit(solution)/shard_map/ppermute | solution.py:31
  114.3 24.6 %collective-permute-start.15 = (bf16[2,8,16,512]{3,2,1,0:T(8,128)(2,1)}, bf16[2,8,16,512]{3,2,1,0:T(8,128)(2,1)}, u32[]{:S(2)}, u32[]{:S(2)}) collective-permute-start(bf16[2,8,16,512]{3,2,1,0:T(8,128)(2,1)} %get-tuple-element.26), channel_id=1, source_target_pairs={{0,128},{32,160},{64,192},{96,224},{128,0},{160,32},{192,64},{224,... | collective-permute-start | bytes 786440 | tf_op jit(solution)/shard_map/ppermute | solution.py:31
  114.4 47.4 %copy-start = (bf16[8,2,4,16,512]{4,3,2,1,0:T(8,128)(2,1)}, bf16[8,2,4,16,512]{4,3,2,1,0:T(8,128)(2,1)S(1)}, u32[]{:S(2)}) copy-start(bf16[8,2,4,16,512]{4,3,2,1,0:T(8,128)(2,1)S(1)} %all-to-all-done.2.bases.rest_0_) | copy-start | bytes 3145732
  114.4 26.3 %collective-permute-start.18 = (bf16[8,4,16,512]{3,2,1,0:T(8,128)(2,1)S(1)}, bf16[8,4,16,512]{3,2,1,0:T(8,128)(2,1)S(1)}, u32[]{:S(2)}, u32[]{:S(2)}) collective-permute-start(bf16[8,4,16,512]{3,2,1,0:T(8,128)(2,1)S(1)} %slice_bitcast_fusion), channel_id=1, source_target_pairs={{0,128},{32,160},{64,192},{96,224},{128,0},{160,32},{192,64},{224,... | collective-permute-start | bytes 1572872 | tf_op jit(solution)/shard_map/ppermute | solution.py:31
  137.4 15.7 %copy-start.9 = (bf16[2,8,16,512]{3,2,1,0:T(8,128)(2,1)}, bf16[2,8,16,512]{3,2,1,0:T(8,128)(2,1)S(1)}, u32[]{:S(2)}) copy-start(bf16[2,8,16,512]{3,2,1,0:T(8,128)(2,1)S(1)} %collective-permute-done.13.e1) | copy-start | bytes 786436
  137.4 12.4 %collective-permute-start.17 = (bf16[8,4,16,512]{3,2,1,0:T(8,128)(2,1)S(1)}, bf16[8,4,16,512]{3,2,1,0:T(8,128)(2,1)}, u32[]{:S(2)}, u32[]{:S(2)}) collective-permute-start(bf16[8,4,16,512]{3,2,1,0:T(8,128)(2,1)S(1)} %slice_bitcast_fusion), channel_id=1, source_target_pairs={{0,192},{32,224},{64,0},{96,32},{128,64},{160,96},{192,128},{224,1... | collective-permute-start | bytes 1572872 | tf_op jit(solution)/shard_map/ppermute | solution.py:31
  137.4 14.4 %collective-permute-start.16 = (bf16[8,4,16,512]{3,2,1,0:T(8,128)(2,1)S(1)}, bf16[8,4,16,512]{3,2,1,0:T(8,128)(2,1)}, u32[]{:S(2)}, u32[]{:S(2)}) collective-permute-start(bf16[8,4,16,512]{3,2,1,0:T(8,128)(2,1)S(1)} %slice_bitcast_fusion), channel_id=1, source_target_pairs={{0,64},{32,96},{64,128},{96,160},{128,192},{160,224},{192,0},{224,... | collective-permute-start | bytes 1572872 | tf_op jit(solution)/shard_map/ppermute | solution.py:31
  138.9 37.5 %collective-permute-start.22 = (bf16[8,2,4,16,512]{4,3,2,1,0:T(8,128)(2,1)S(1)}, bf16[8,2,4,16,512]{4,3,2,1,0:T(8,128)(2,1)}, u32[]{:S(2)}, u32[]{:S(2)}) collective-permute-start(bf16[8,2,4,16,512]{4,3,2,1,0:T(8,128)(2,1)S(1)} %all-to-all-done.2.bases.rest_0_), channel_id=1, source_target_pairs={{0,32},{32,0},{64,96},{96,64},{128,160},{160,128},{192,224},{224,1... | collective-permute-start | bytes 3145736 | tf_op jit(solution)/shard_map/ppermute | solution.py:36
  140.7 27.8 %copy-start.5 = (bf16[8,4,16,512]{3,2,1,0:T(8,128)(2,1)}, bf16[8,4,16,512]{3,2,1,0:T(8,128)(2,1)S(1)}, u32[]{:S(2)}) copy-start(bf16[8,4,16,512]{3,2,1,0:T(8,128)(2,1)S(1)} %collective-permute-done.18.rest_3_) | copy-start | bytes 1572868
  140.7 35.7 %collective-permute-start.25 = (bf16[8,4,16,512]{3,2,1,0:T(8,128)(2,1)S(1)}, bf16[8,4,16,512]{3,2,1,0:T(8,128)(2,1)}, u32[]{:S(2)}, u32[]{:S(2)}) collective-permute-start(bf16[8,4,16,512]{3,2,1,0:T(8,128)(2,1)S(1)} %collective-permute-done.18.rest_3_), channel_id=1, source_target_pairs={{0,32},{32,0},{64,96},{96,64},{128,160},{160,128},{192,224},{224,1... | collective-permute-start | bytes 1572872 | tf_op jit(solution)/shard_map/ppermute | solution.py:36
  149.8 26.6 %collective-permute-start.24 = (bf16[8,4,16,512]{3,2,1,0:T(8,128)(2,1)}, bf16[8,4,16,512]{3,2,1,0:T(8,128)(2,1)}, u32[]{:S(2)}, u32[]{:S(2)}) collective-permute-start(bf16[8,4,16,512]{3,2,1,0:T(8,128)(2,1)} %collective-permute-done.17.rest_2_), channel_id=1, source_target_pairs={{0,32},{32,0},{64,96},{96,64},{128,160},{160,128},{192,224},{224,1... | collective-permute-start | bytes 1572872 | tf_op jit(solution)/shard_map/ppermute | solution.py:36
  151.9 24.5 %collective-permute-start.23 = (bf16[8,4,16,512]{3,2,1,0:T(8,128)(2,1)}, bf16[8,4,16,512]{3,2,1,0:T(8,128)(2,1)}, u32[]{:S(2)}, u32[]{:S(2)}) collective-permute-start(bf16[8,4,16,512]{3,2,1,0:T(8,128)(2,1)} %collective-permute-done.16.rest_1_), channel_id=1, source_target_pairs={{0,32},{32,0},{64,96},{96,64},{128,160},{160,128},{192,224},{224,1... | collective-permute-start | bytes 1572872 | tf_op jit(solution)/shard_map/ppermute | solution.py:36
  155.3 18.8 %all-to-all-start.1 = ((bf16[8,2,16,512]{3,2,1,0:T(8,128)(2,1)}), bf16[8,2,16,512]{3,2,1,0:T(8,128)(2,1)S(1)}, u32[]{:S(2)}, u32[]{:S(2)}) async-start(bf16[8,2,16,512]{3,2,1,0:T(8,128)(2,1)} %over_x.1), calls=%async_computation.1 | async-start | bytes 524288 | tf_op jit(solution)/shard_map/all_to_all | solution.py:41
  174.1 0.7 copy-start.3
